TPU v7x, 32 devices: a whole 2x2x4 slice. The times are simulated.
32 devices in a mesh: rows: 8 (over y, x, core), chan: 4 (over z).
Axes of the slice: x: 2, y: 2, z: 4, core: 2. Of those that a mesh axis runs over, the one named last changes fastest.
Arguments:
- features: bfloat16 [1024, 1, 4096], P('chan', None, 'rows'), may hold values from -24 to 24
- gain_first: float32 [1024], P('chan'), may hold values from 0.1 to 1.9
- weight_first: bfloat16 [3, 3, 3, 1024, 1024], P(None, None, None, 'chan'), may hold values from -0.0390625 to 0.0390625
- bias_first: float32 [1024], P('chan'), may hold values from -3 to 3
- gain_second: float32 [1024], P('chan'), may hold values from 0.1 to 1.9
- weight_second: bfloat16 [3, 3, 3, 1024, 1024], P(None, None, None, 'chan'), may hold values from -0.0390625 to 0.0390625
- bias_second: float32 [1024], P('chan'), may hold values from -3 to 3
Outputs:
- block_out: bfloat16 [1024, 1, 4096], P('chan', None, 'rows')
All inputs are finite; a program needn't handle non-finite values.
Results may differ from a plain program's by a relative error of at most 0.0022.
Values may be sent and summed in bfloat16 or wider, within the bound.
No kernel may reach another device: no remote copies, remote signals or barrier semaphores. Data moves between devices by JAX's collectives and lax.ppermute only.
A program may use at most 64 MiB of HBM per device.

v0:
```python
import jax
import jax.numpy as jnp
from jax import lax
from jax.experimental import pallas as pl
from jax.experimental.pallas import tpu as pltpu
from jax.sharding import PartitionSpec as P

WIDTH = 64
LANES = 128


def shift_along(block, axis, step):
    count = lax.axis_size(axis)
    pairs = [(i, i + step) for i in range(count) if 0 <= i + step < count]
    return lax.ppermute(block, axis, pairs)


VMEM = pl.BlockSpec(memory_space=pltpu.VMEM)
HBM = pl.BlockSpec(memory_space=pltpu.HBM)
PARAMS = pltpu.CompilerParams(vmem_limit_bytes=20 << 20)


def column_of(row):
    return jnp.broadcast_to(row, (LANES, row.shape[1])).T[:, :1]


def row_of(column):
    return jnp.broadcast_to(column, (column.shape[0], LANES)).T[:1]


def silu(values):
    return values / (1.0 + jnp.exp(-values))


def filter_copies(frame, weights, taps, sems):
    return [
        pltpu.make_async_copy(weights.at[frame, q, s], taps.at[q * 3 + s], sems.at[q * 3 + s])
        for q in range(3)
        for s in range(3)
    ]


def fetch_kernel(frame, weights, taps, sems):
    copies = filter_copies(frame, weights, taps, sems)
    for copy in copies:
        copy.start()
    for copy in copies:
        copy.wait()


def fetch(weights):
    outs, total = weights.shape[3:]
    return pl.pallas_call(
        lambda *refs: fetch_kernel(weights.shape[0] - 1, *refs),
        out_shape=pltpu.VMEM((9, outs, total), weights.dtype),
        in_specs=[HBM],
        out_specs=VMEM,
        scratch_shapes=[pltpu.SemaphoreType.DMA((9,))],
        compiler_params=PARAMS,
    )(pltpu.with_memory_space_constraint(weights, pltpu.HBM))


def shifted(values):
    cells = values.shape[0]
    column = lax.broadcasted_iota(jnp.int32, (cells, 1), 0) % WIDTH
    before = jnp.where(column == 0, 0.0, pltpu.roll(values, 1, 0))
    after = jnp.where(column == WIDTH - 1, 0.0, pltpu.roll(values, cells - 1, 0))
    return [part.astype(jnp.bfloat16) for part in (before, values, after)]


def matmul(left, right):
    return lax.dot_general(
        jnp.concatenate(left, axis=1),
        jnp.concatenate(right, axis=1),
        (((1,), (1,)), ((), ())),
        preferred_element_type=jnp.float32,
    )


def steps_of(count):
    return sorted(range(1, count), key=lambda step: (step != count // 2, step))


def owner_of(k):
    return lax.axis_index("chan") ^ [0, *steps_of(lax.axis_size("chan"))][k]


def lanes_of(owner, width):
    return pl.ds(pl.multiple_of(owner * width, width), width)


def main_taps(block, taps, owner, acts):
    cells, width = block.shape
    zeros = jnp.zeros((WIDTH, width), acts.dtype)
    for s, part in enumerate(shifted(block.astype(jnp.float32))):
        acts[s, :WIDTH] = zeros
        acts[s, WIDTH : WIDTH + cells] = part
        acts[s, WIDTH + cells :] = zeros
    lanes = lanes_of(owner, width)
    left = [acts[s, q * WIDTH : q * WIDTH + cells] for q in range(3) for s in range(3)]
    return matmul(left, [taps[t, :, lanes] for t in range(9)])


def edge_taps(block, taps, owner):
    cells, width = block.shape
    lanes = lanes_of(owner, width)
    above = matmul(shifted(block[:WIDTH].astype(jnp.float32)), [taps[6 + s, :, lanes] for s in range(3)])
    low = shifted(block[cells - WIDTH :].astype(jnp.float32))
    return above, matmul(low, [taps[s, :, lanes] for s in range(3)])


def gain_rows(parts, lanes, rows):
    width = parts[0].shape[1]
    step = min(width, lanes)
    pieces = [part[:, k : k + step] for part in parts for k in range(0, width, step)]
    result = jnp.concatenate([*pieces, jnp.zeros((rows - len(pieces), step), jnp.float32)], axis=0)
    if lanes > step:
        result = jnp.concatenate([result, jnp.zeros((rows, lanes - step), jnp.float32)], axis=1)
    return result


def gain_from(note, width):
    step = min(width, note.shape[1])
    count = width // step
    rows = [note[k : k + 1, :step].astype(jnp.float32) for k in range(3 * count)]
    parts = [jnp.concatenate(rows[k * count : (k + 1) * count], axis=1) for k in range(3)]
    return (parts[0] + parts[1]) + parts[2]


def send_kernel(source, note, whole, edge, body, gain, sems):
    width, cells = source.shape
    copies = [
        pltpu.make_async_copy(source, whole.at[:width], sems.at[0]),
        pltpu.make_async_copy(note, gain, sems.at[1]),
    ]
    for copy in copies:
        copy.start()
    copies[1].wait()
    parts, rest = [], gain[...]
    for _ in range(3):
        parts.append(rest.astype(jnp.bfloat16).astype(jnp.float32))
        rest = rest - parts[-1]
    for out in (whole, edge):
        out[width:] = gain_rows(parts, out.shape[1], out.shape[0] - width).astype(out.dtype)
    copies[0].wait()
    edge[:width] = edges_in(whole[:width])
    body[...] = whole[:width, WIDTH : cells - WIDTH]


def edges_in(block):
    cells = block.shape[1]
    return jnp.concatenate([block[:, :WIDTH], block[:, cells - WIDTH :]], axis=1)


def to_send(block, gain):
    width, cells = block.shape
    pieces = 3 * pl.cdiv(width, 2 * WIDTH)
    shapes = [(width + 8, cells), (width + 8 * pl.cdiv(pieces, 8), 2 * WIDTH), (width, cells - 2 * WIDTH)]
    return pl.pallas_call(
        send_kernel,
        out_shape=[pltpu.VMEM(shape, block.dtype) for shape in shapes],
        in_specs=[HBM] * 2,
        out_specs=[VMEM] * 3,
        scratch_shapes=[pltpu.VMEM(gain.shape, gain.dtype), pltpu.SemaphoreType.DMA((2,))],
        compiler_params=PARAMS,
    )(*[pltpu.with_memory_space_constraint(value, pltpu.HBM) for value in (block, gain)])


def normed(values, gains, total):
    values = [value.astype(jnp.float32) for value in values]
    squares = sum(jnp.sum(value * value, axis=0, keepdims=True) for value in values)
    inverse = column_of(1.0 / jnp.sqrt(squares / total + 1e-6))
    return [silu(value.T * gain * inverse).astype(jnp.bfloat16) for value, gain in zip(values, gains)]


def first_gains(wholes, edge, width):
    return [gain_from(ref[width:], width) for ref in (*wholes, edge)]


def first_edge_kernel(total, *refs):
    wholes, (edge, taps, first, second) = refs[:-4], refs[-4:]
    width = wholes[0].shape[0] - 8
    values = [edges_in(ref[:width]) for ref in wholes] + [edge[:width]]
    blocks = normed(values, first_gains(wholes, edge, width), total)
    parts = [edge_taps(block, taps, owner_of(k)) for k, block in enumerate(blocks)]
    first[...], second[...] = to_swap(sum(p[0] for p in parts), sum(p[1] for p in parts))


def first_edge(wholes, edge, taps):
    outs, total = taps.shape[1:]
    return pl.pallas_call(
        lambda *refs: first_edge_kernel(total, *refs),
        out_shape=[jax.ShapeDtypeStruct((WIDTH, outs), jnp.float32)] * 2,
        in_specs=[VMEM] * (len(wholes) + 2),
        out_specs=[VMEM] * 2,
        compiler_params=PARAMS,
    )(*wholes, edge, taps)


def first_kernel(total, *refs):
    wholes, (edge, body, taps, out, blocks, acts) = refs[:-6], refs[-6:]
    width = wholes[0].shape[0] - 8
    ends = edge[:width]
    last = jnp.concatenate([ends[:, :WIDTH], body[...], ends[:, WIDTH:]], axis=1)
    values = [ref[:width] for ref in wholes] + [last]
    for k, block in enumerate(normed(values, first_gains(wholes, edge, width), total)):
        blocks[k] = block
    for k in range(len(values)):
        part = main_taps(blocks[k], taps, owner_of(k), acts.at[k % 2])
        out[...] = part if k == 0 else out[...] + part


def first_main(wholes, edge, body, taps):
    outs, total = taps.shape[1:]
    width, cells = wholes[0].shape[0] - 8, wholes[0].shape[1]
    return pl.pallas_call(
        lambda *refs: first_kernel(total, *refs),
        out_shape=jax.ShapeDtypeStruct((cells, outs), jnp.float32),
        in_specs=[VMEM] * (len(wholes) + 3),
        out_specs=VMEM,
        scratch_shapes=[
            pltpu.VMEM((len(wholes) + 1, cells, width), jnp.bfloat16),
            pltpu.VMEM((2, 3, cells + 2 * WIDTH, width), jnp.bfloat16),
        ],
        compiler_params=PARAMS,
    )(*wholes, edge, body, taps)


def part_kernel(k, block, taps, *refs):
    before, outs, acts = refs[:-4], refs[-4:-1], refs[-1]
    parts = [main_taps(block[...], taps, owner_of(k), acts), *edge_taps(block[...], taps, owner_of(k))]
    for place, part in enumerate(parts):
        outs[place][...] = before[place][...] + part if before else part


def second_part(k, block, taps, before):
    cells, width = block.shape
    outs = taps.shape[1]
    return pl.pallas_call(
        lambda *refs: part_kernel(k, *refs),
        out_shape=[jax.ShapeDtypeStruct((size, outs), jnp.float32) for size in (cells, WIDTH, WIDTH)],
        in_specs=[VMEM] * (2 + len(before)),
        out_specs=[VMEM] * 3,
        input_output_aliases={2 + i: i for i in range(len(before))},
        scratch_shapes=[pltpu.VMEM((3, cells + 2 * WIDTH, width), jnp.bfloat16)],
        compiler_params=PARAMS,
    )(block, taps, *before)


def second_edge_kernel(k, edge, taps, above, below, first, second):
    parts = edge_taps(edge[...], taps, owner_of(k))
    first[...], second[...] = to_swap(above[...] + parts[0], below[...] + parts[1])


def second_edge(k, edge, taps, above, below):
    return pl.pallas_call(
        lambda *refs: second_edge_kernel(k, *refs),
        out_shape=[jax.ShapeDtypeStruct(above.shape, above.dtype)] * 2,
        in_specs=[VMEM] * 4,
        out_specs=[VMEM] * 2,
        compiler_params=PARAMS,
    )(edge, taps, above, below)


def second_main_kernel(k, edge, body, taps, before, out, acts):
    block = jnp.concatenate([edge[:WIDTH], body[...], edge[WIDTH:]], axis=0)
    out[...] = before[...] + main_taps(block, taps, owner_of(k), acts)


def second_main(k, edge, body, taps, before):
    return pl.pallas_call(
        lambda *refs: second_main_kernel(k, *refs),
        out_shape=jax.ShapeDtypeStruct(before.shape, before.dtype),
        in_specs=[VMEM] * 4,
        out_specs=VMEM,
        input_output_aliases={3: 0},
        scratch_shapes=[pltpu.VMEM((3, before.shape[0] + 2 * WIDTH, edge.shape[1]), jnp.bfloat16)],
        compiler_params=PARAMS,
    )(edge, body, taps, before)


def to_swap(above, below):
    even = lax.axis_index("rows") % 2 == 0
    return jnp.where(even, below, above), jnp.where(even, above, below)


def joined(main, first, second, bias):
    row = lax.axis_index("rows")
    even, top, low = row % 2 == 0, row == 0, row == lax.axis_size("rows") - 1
    above = jnp.where(even, second[...], first[...])
    below = jnp.where(even, first[...], second[...])
    above, below = jnp.where(top, 0.0, above), jnp.where(low, 0.0, below)
    end = main.shape[0] - WIDTH
    rows = [main[:WIDTH] + above, main[WIDTH:end], main[end:] + below]
    return jnp.concatenate(rows, axis=0) + bias[...]


def middle_kernel(main, first, second, bias, out, squares):
    middle = joined(main, first, second, bias)
    out[...] = middle
    squares[...] = row_of(jnp.sum(middle * middle, axis=1, keepdims=True))


def out_kernel(main, first, second, bias, source, out):
    result = joined(main, first, second, bias).T + source[...].astype(jnp.float32)
    out[...] = result.astype(out.dtype)


def act_kernel(total, values, gain, *refs):
    sums, (out, edge, body) = refs[:-3], refs[-3:]
    inverse = column_of(1.0 / jnp.sqrt(sum(ref[...] for ref in sums) / total + 1e-6))
    result = silu(values[...] * gain[...] * inverse).astype(out.dtype)
    end = result.shape[0] - WIDTH
    out[...] = result
    edge[:WIDTH], edge[WIDTH:] = result[:WIDTH], result[end:]
    body[...] = result[WIDTH:end]


def act(values, gain, sums, total):
    return pl.pallas_call(
        lambda *refs: act_kernel(total, *refs),
        out_shape=[
            jax.ShapeDtypeStruct((size, values.shape[1]), jnp.bfloat16)
            for size in (values.shape[0], 2 * WIDTH, values.shape[0] - 2 * WIDTH)
        ],
        in_specs=[VMEM] * (2 + len(sums)),
        out_specs=[VMEM] * 3,
        compiler_params=PARAMS,
    )(values, gain, *sums)


def with_row_neighbours(sends):
    count = lax.axis_size("rows")
    rounds = []
    for begin, send in enumerate(sends):
        pairs = [(i, (i + 1) % count) for i in range(begin, count, 2)]
        rounds.append(lax.ppermute(send, "rows", pairs + [(b, a) for a, b in pairs]))
    return rounds


def swap(value, step):
    return lax.ppermute(value, "chan", [(i, i ^ step) for i in range(lax.axis_size("chan"))])


def gathered(block, edge, body):
    *steps, last = steps_of(lax.axis_size("chan"))
    blocks = [block] + [swap(block, step) for step in steps]
    return blocks, *[swap(v, last) for v in (edge, body)]


def resident(
    features, gain_first, weight_first, bias_first, gain_second, weight_second, bias_second
):
    channels, frames, cells = features.shape
    total = weight_first.shape[4]
    count = lax.axis_size("chan")
    source = features.reshape(channels, cells)
    taps = fetch(weight_first)
    blocks, edge, body = gathered(*to_send(source, gain_first.reshape(1, -1)))
    sends = first_edge(blocks, edge, taps)
    edges = with_row_neighbours(sends)
    main = first_main(blocks, edge, body, taps)
    middle, squares = pl.pallas_call(
        middle_kernel,
        out_shape=[
            jax.ShapeDtypeStruct((cells, channels), jnp.float32),
            jax.ShapeDtypeStruct((1, cells), jnp.float32),
        ],
        in_specs=[VMEM] * 4,
        out_specs=[VMEM] * 2,
        compiler_params=PARAMS,
    )(main, *edges, bias_first.reshape(1, -1))
    others = [swap(squares, step) for step in range(count - 1, 0, -1)]
    second = act(middle, gain_second.reshape(1, -1), [squares, *others], total)
    taps = fetch(weight_second)
    blocks, edge, body = gathered(*second)
    parts = ()
    for k, block in enumerate(blocks):
        parts = second_part(k, block, taps, parts)
    sends = second_edge(count - 1, edge, taps, *parts[1:])
    edges = with_row_neighbours(sends)
    main = second_main(count - 1, edge, body, taps, parts[0])
    out = pl.pallas_call(
        out_kernel,
        out_shape=jax.ShapeDtypeStruct((channels, cells), features.dtype),
        in_specs=[VMEM] * 5,
        out_specs=VMEM,
        compiler_params=PARAMS,
    )(main, *edges, bias_second.reshape(1, -1), source)
    return out.reshape(channels, frames, cells)


def padded(block, width):
    low = shift_along(block[..., block.shape[-1] - width :], "rows", 1)
    high = shift_along(block[..., :width], "rows", -1)
    return jnp.concatenate([low, block, high], axis=-1)


def activate(values, gain, total):
    mean_sq = lax.psum(jnp.sum(values * values, axis=0, keepdims=True), "chan") / total
    return jax.nn.silu(values * gain[:, None, None] / jnp.sqrt(mean_sq + 1e-06)).astype(jnp.bfloat16)


def convolve(block, kernel):
    whole = padded(lax.all_gather(block, "chan", axis=0, tiled=True), WIDTH)
    channels, frames, cells = whole.shape
    grid = whole.reshape(1, channels, frames, cells // WIDTH, WIDTH)
    result = lax.conv_general_dilated(
        grid,
        kernel,
        (1, 1, 1),
        ((2, 0), (0, 0), (1, 1)),
        dimension_numbers=("NCDHW", "DHWOI", "NCDHW"),
        preferred_element_type=jnp.float32,
    )
    return result[0].reshape(kernel.shape[3], frames, cells - 2 * WIDTH)


def general(features, gain_first, weight_first, bias_first, gain_second, weight_second, bias_second):
    total = weight_first.shape[4]
    source = features.astype(jnp.float32)
    middle = convolve(activate(source, gain_first, total), weight_first) + bias_first[:, None, None]
    result = convolve(activate(middle, gain_second, total), weight_second)
    return (source + result + bias_second[:, None, None]).astype(jnp.bfloat16)


def on_device(
    features, gain_first, weight_first, bias_first, gain_second, weight_second, bias_second
):
    channels, frames, cells = features.shape
    chan, rows = lax.axis_size("chan"), lax.axis_size("rows")
    narrow = channels % LANES or cells < 3 * WIDTH or channels > cells
    if frames != 1 or narrow or chan < 2 or chan & (chan - 1) or rows % 2:
        return general(
            features, gain_first, weight_first, bias_first, gain_second, weight_second, bias_second
        )
    out = resident(
        features, gain_first, weight_first, bias_first, gain_second, weight_second, bias_second
    )
    return out


def solution(mesh):
    in_specs = (
        P("chan", None, "rows"),
        P("chan"),
        P(None, None, None, "chan", None),
        P("chan"),
        P("chan"),
        P(None, None, None, "chan", None),
        P("chan"),
    )
    return jax.shard_map(
        on_device, mesh=mesh, in_specs=in_specs, out_specs=P("chan", None, "rows"), check_vma=False
    )
```

profile of v0, /device:TPU:9, one launch (start us, length us, event | category | flops | bytes accessed | tf_op | source)
XLA Modules:
  0.0 71.2 jit_solution(12404638078684650160)
XLA Ops:
  0.0 1.1 %shard_map.73 = (bf16[264,512]{1,0:T(8,128)(2,1)S(1)}, bf16[264,128]{1,0:T(8,128)(2,1)S(1)}, bf16[256,384]{1,0:T(8,128)(2,1)S(1)}) custom-call(bf16[256,512]{1,0:T(8,128)(2,1)} %bitcast.6, f32[1,256]{1,0:T(1,128)} %bitcast.11), custom_call_target="tpu_custom_call" | custom-call | tf_op jit(solution)/shard_map/pallas_call | solution.py:159
  1.1 2.4 %collective-permute-start = (bf16[264,512]{1,0:T(8,128)(2,1)S(1)}, bf16[264,512]{1,0:T(8,128)(2,1)S(1)}, u32[]{:S(2)}, u32[]{:S(2)}) collective-permute-start(bf16[264,512]{1,0:T(8,128)(2,1)S(1)} %get-tuple-element.26.refs_0_), channel_id=1, source_target_pairs={{0,2},{1,3},{2,0},{3,1},{4,6},{5,7},{6,4},{7,5},{8,10},{9,11},{10,... | collective-permute-start | bytes 811016 | tf_op jit(solution)/shard_map/ppermute | solution.py:342
  3.5 0.2 collective-permute-start.1
  3.7 0.2 collective-permute-start.3
  3.9 1.3 %collective-permute-start.2 = (bf16[264,128]{1,0:T(8,128)(2,1)S(1)}, bf16[264,128]{1,0:T(8,128)(2,1)S(1)}, u32[]{:S(2)}, u32[]{:S(2)}) collective-permute-start(bf16[264,128]{1,0:T(8,128)(2,1)S(1)} %get-tuple-element.27), channel_id=1, source_target_pairs={{0,3},{1,2},{2,1},{3,0},{4,7},{5,6},{6,5},{7,4},{8,11},{9,10},{10,... | collective-permute-start | bytes 202760 | tf_op jit(solution)/shard_map/ppermute | solution.py:342
  5.1 2.4 %shard_map.74.refs_5_.refs_4_ = bf16[9,256,1024]{2,1,0:T(8,128)(2,1)S(1)} custom-call(bf16[3,3,3,256,1024]{4,3,2,1,0:T(8,128)(2,1)} %refs_0_.2), custom_call_target="tpu_custom_call" | custom-call | tf_op jit(solution)/shard_map/pallas_call | solution.py:53
  7.5 19.2 %collective-permute-done.2.refs_3_ = bf16[264,128]{1,0:T(8,128)(2,1)S(1)} collective-permute-done((bf16[264,128]{1,0:T(8,128)(2,1)S(1)}, bf16[264,128]{1,0:T(8,128)(2,1)S(1)}, u32[]{:S(2)}, u32[]{:S(2)}) %collective-permute-start.2) | collective-permute-done | bytes 67616 | tf_op jit(solution)/shard_map/ppermute | solution.py:342
  26.7 0.0 collective-permute-done.refs_1_
  26.7 0.0 collective-permute-done.1.refs_2_
  26.7 1.2 %shard_map.76 = (f32[64,256]{1,0:T(8,128)S(1)}, f32[64,256]{1,0:T(8,128)S(1)}) custom-call(bf16[264,512]{1,0:T(8,128)(2,1)S(1)} %get-tuple-element.26.refs_0_, bf16[264,512]{1,0:T(8,128)(2,1)S(1)} %collective-permute-done.refs_1_, bf16[264,512]{1,0:T(8,128)(2,1)S(1)} %collective-permute-done.1.refs_2_, bf16[264,128]{1,0:T(8,128)(2,1)S(1)} %collective-permute-done.2.refs_3_, ...), custom_call_target="tpu_custom_call" | custom-call | tf_op jit(solution)/shard_map/pallas_call | solution.py:191
  27.9 0.6 collective-permute-start.4
  28.5 1.2 %collective-permute-start.5 = (f32[64,256]{1,0:T(8,128)S(1)}, f32[64,256]{1,0:T(8,128)S(1)}, u32[]{:S(2)}, u32[]{:S(2)}) collective-permute-start(f32[64,256]{1,0:T(8,128)S(1)} %get-tuple-element.30), channel_id=1, source_target_pairs={{4,8},{12,16},{20,24},{28,0},{8,4},{16,12},{24,20},{0,28},{5,9},{1... | collective-permute-start | bytes 196616 | tf_op jit(solution)/shard_map/ppermute | solution.py:337
  29.7 0.0 collective-permute-done.3.refs_4_
  29.7 3.4 %shard_map.75.main = f32[512,256]{1,0:T(8,128)S(1)} custom-call(bf16[264,512]{1,0:T(8,128)(2,1)S(1)} %get-tuple-element.26.refs_0_, bf16[264,512]{1,0:T(8,128)(2,1)S(1)} %collective-permute-done.refs_1_, bf16[264,512]{1,0:T(8,128)(2,1)S(1)} %collective-permute-done.1.refs_2_, bf16[264,128]{1,0:T(8,128)(2,1)S(1)} %collective-permute-done.2.refs_3_, ...), custom_call_target="tpu_custom_call" | custom-call | tf_op jit(solution)/shard_map/pallas_call | solution.py:216
  33.1 0.0 collective-permute-done.4.first
  33.1 0.0 collective-permute-done.5.second
  33.1 0.0 copy-done.1
  33.1 0.2 shard_map.77
  33.3 2.3 %collective-permute-start.6 = (f32[1,512]{1,0:T(1,128)S(1)}, f32[1,512]{1,0:T(1,128)S(1)}, u32[]{:S(2)}, u32[]{:S(2)}) collective-permute-start(f32[1,512]{1,0:T(1,128)S(1)} %get-tuple-element.32.refs_2_), channel_id=1, source_target_pairs={{0,3},{1,2},{2,1},{3,0},{4,7},{5,6},{6,5},{7,4},{8,11},{9,10},{10,... | collective-permute-start | bytes 6152 | tf_op jit(solution)/shard_map/ppermute | solution.py:342
  35.6 0.0 collective-permute-start.7
  35.6 1.3 %collective-permute-start.8 = (f32[1,512]{1,0:T(1,128)S(1)}, f32[1,512]{1,0:T(1,128)S(1)}, u32[]{:S(2)}, u32[]{:S(2)}) collective-permute-start(f32[1,512]{1,0:T(1,128)S(1)} %get-tuple-element.32.refs_2_), channel_id=1, source_target_pairs={{0,1},{1,0},{2,3},{3,2},{4,5},{5,4},{6,7},{7,6},{8,9},{9,8},{10,11... | collective-permute-start | bytes 6152 | tf_op jit(solution)/shard_map/ppermute | solution.py:342
  36.8 0.0 collective-permute-done.6.refs_3_
  36.8 2.1 %collective-permute-done.7.refs_4_ = f32[1,512]{1,0:T(1,128)S(1)} collective-permute-done((f32[1,512]{1,0:T(1,128)S(1)}, f32[1,512]{1,0:T(1,128)S(1)}, u32[]{:S(2)}, u32[]{:S(2)}) %collective-permute-start.7) | collective-permute-done | bytes 2080 | tf_op jit(solution)/shard_map/ppermute | solution.py:342
  38.9 0.0 collective-permute-done.8.refs_5_
  38.9 0.0 copy-done.2
  38.9 0.3 shard_map.78
  39.3 1.8 %collective-permute-start.12 = (bf16[512,256]{1,0:T(8,128)(2,1)S(1)}, bf16[512,256]{1,0:T(8,128)(2,1)S(1)}, u32[]{:S(2)}, u32[]{:S(2)}) collective-permute-start(bf16[512,256]{1,0:T(8,128)(2,1)S(1)} %get-tuple-element.35.refs_0_), channel_id=1, source_target_pairs={{0,2},{1,3},{2,0},{3,1},{4,6},{5,7},{6,4},{7,5},{8,10},{9,11},{10,... | collective-permute-start | bytes 786440 | tf_op jit(solution)/shard_map/ppermute | solution.py:342
  41.1 0.0 collective-permute-start.11
  41.1 0.9 %collective-permute-start.10 = (bf16[384,256]{1,0:T(8,128)(2,1)S(1)}, bf16[384,256]{1,0:T(8,128)(2,1)S(1)}, u32[]{:S(2)}, u32[]{:S(2)}) collective-permute-start(bf16[384,256]{1,0:T(8,128)(2,1)S(1)} %get-tuple-element.34), channel_id=1, source_target_pairs={{0,3},{1,2},{2,1},{3,0},{4,7},{5,6},{6,5},{7,4},{8,11},{9,10},{10,... | collective-permute-start | bytes 589832 | tf_op jit(solution)/shard_map/ppermute | solution.py:342
  42.0 0.6 collective-permute-start.9
  42.6 2.4 %shard_map.79.refs_1_.refs_2_ = bf16[9,256,1024]{2,1,0:T(8,128)(2,1)S(1)} custom-call(bf16[3,3,3,256,1024]{4,3,2,1,0:T(8,128)(2,1)} %refs_0_.3), custom_call_target="tpu_custom_call" | custom-call | tf_op jit(solution)/shard_map/pallas_call | solution.py:53
  44.9 0.0 copy-start
  45.0 0.0 copy-start.3
  45.0 1.0 %shard_map.80 = (f32[512,256]{1,0:T(8,128)S(1)}, f32[64,256]{1,0:T(8,128)S(1)}, f32[64,256]{1,0:T(8,128)S(1)}) custom-call(bf16[512,256]{1,0:T(8,128)(2,1)S(1)} %get-tuple-element.35.refs_0_, bf16[9,256,1024]{2,1,0:T(8,128)(2,1)S(1)} %shard_map.79.refs_1_.refs_2_), custom_call_target="tpu_custom_call" | custom-call | tf_op jit(solution)/shard_map/pallas_call | solution.py:239
  46.0 7.5 %collective-permute-done.12.refs_0_ = bf16[512,256]{1,0:T(8,128)(2,1)S(1)} collective-permute-done((bf16[512,256]{1,0:T(8,128)(2,1)S(1)}, bf16[512,256]{1,0:T(8,128)(2,1)S(1)}, u32[]{:S(2)}, u32[]{:S(2)}) %collective-permute-start.12) | collective-permute-done | bytes 262176 | tf_op jit(solution)/shard_map/ppermute | solution.py:342
  53.5 1.0 %shard_map.81 = (f32[512,256]{1,0:T(8,128)S(1)}, f32[64,256]{1,0:T(8,128)S(1)}, f32[64,256]{1,0:T(8,128)S(1)}) custom-call(bf16[512,256]{1,0:T(8,128)(2,1)S(1)} %collective-permute-done.12.refs_0_, bf16[9,256,1024]{2,1,0:T(8,128)(2,1)S(1)} %shard_map.79.refs_1_.refs_2_, ...), custom_call_target="tpu_custom_call", output_to_operand_aliasing={{0}: (2, {}), {1}: (3, {}), {2}: (4, {})} | custom-call | tf_op jit(solution)/shard_map/pallas_call | solution.py:239
  54.5 0.0 collective-permute-done.11.refs_0_
  54.6 1.0 %shard_map.82 = (f32[512,256]{1,0:T(8,128)S(1)}, f32[64,256]{1,0:T(8,128)S(1)}, f32[64,256]{1,0:T(8,128)S(1)}) custom-call(bf16[512,256]{1,0:T(8,128)(2,1)S(1)} %collective-permute-done.11.refs_0_, bf16[9,256,1024]{2,1,0:T(8,128)(2,1)S(1)} %shard_map.79.refs_1_.refs_2_, ...), custom_call_target="tpu_custom_call", output_to_operand_aliasing={{0}: (2, {}), {1}: (3, {}), {2}: (4, {})} | custom-call | tf_op jit(solution)/shard_map/pallas_call | solution.py:239
  55.6 8.6 %collective-permute-done.9.refs_0_ = bf16[128,256]{1,0:T(8,128)(2,1)S(1)} collective-permute-done((bf16[128,256]{1,0:T(8,128)(2,1)S(1)}, bf16[128,256]{1,0:T(8,128)(2,1)S(1)}, u32[]{:S(2)}, u32[]{:S(2)}) %collective-permute-start.9) | collective-permute-done | bytes 65568 | tf_op jit(solution)/shard_map/ppermute | solution.py:342
  64.2 0.4 shard_map.84
  64.6 1.1 %collective-permute-start.13 = (f32[64,256]{1,0:T(8,128)S(1)}, f32[64,256]{1,0:T(8,128)S(1)}, u32[]{:S(2)}, u32[]{:S(2)}) collective-permute-start(f32[64,256]{1,0:T(8,128)S(1)} %get-tuple-element.45), channel_id=1, source_target_pairs={{0,4},{8,12},{16,20},{24,28},{4,0},{12,8},{20,16},{28,24},{1,5},{9... | collective-permute-start | bytes 196616 | tf_op jit(solution)/shard_map/ppermute | solution.py:337
  65.7 1.0 %collective-permute-start.14 = (f32[64,256]{1,0:T(8,128)S(1)}, f32[64,256]{1,0:T(8,128)S(1)}, u32[]{:S(2)}, u32[]{:S(2)}) collective-permute-start(f32[64,256]{1,0:T(8,128)S(1)} %get-tuple-element.46), channel_id=1, source_target_pairs={{4,8},{12,16},{20,24},{28,0},{8,4},{16,12},{24,20},{0,28},{5,9},{1... | collective-permute-start | bytes 196616 | tf_op jit(solution)/shard_map/ppermute | solution.py:337
  66.7 0.0 collective-permute-done.10.refs_1_
  66.7 0.8 %shard_map.83.main = f32[512,256]{1,0:T(8,128)S(1)} custom-call(bf16[128,256]{1,0:T(8,128)(2,1)S(1)} %collective-permute-done.9.refs_0_, bf16[384,256]{1,0:T(8,128)(2,1)S(1)} %collective-permute-done.10.refs_1_, bf16[9,256,1024]{2,1,0:T(8,128)(2,1)S(1)} %shard_map.79.refs_1_.refs_2_, ...), custom_call_target="tpu_custom_call", output_to_operand_aliasing={{}: (3, {})} | custom-call | tf_op jit(solution)/shard_map/pallas_call | solution.py:271
  67.5 0.0 collective-permute-done.13.first
  67.5 2.8 %collective-permute-done.14.second = f32[64,256]{1,0:T(8,128)S(1)} collective-permute-done((f32[64,256]{1,0:T(8,128)S(1)}, f32[64,256]{1,0:T(8,128)S(1)}, u32[]{:S(2)}, u32[]{:S(2)}) %collective-permute-start.14) | collective-permute-done | bytes 65568 | tf_op jit(solution)/shard_map/ppermute | solution.py:337
  70.3 0.0 copy-done.3
  70.3 0.9 %shard_map.85 = bf16[256,512]{1,0:T(8,128)(2,1)} custom-call(f32[512,256]{1,0:T(8,128)S(1)} %shard_map.83.main, f32[64,256]{1,0:T(8,128)S(1)} %collective-permute-done.13.first, f32[64,256]{1,0:T(8,128)S(1)} %collective-permute-done.14.second, f32[1,256]{1,0:T(1,128)S(1)} %bitcast.10, bf16[256,512]{1,0:T(8,128)(2,1)S(1)} %bitcast.7), custom_call_target="tpu_custom_call" | custom-call | tf_op jit(solution)/shard_map/pallas_call | solution.py:383
  (3 shorter events, 0.0 us)
Async XLA Ops:
  1.1 25.6 %collective-permute-start = (bf16[264,512]{1,0:T(8,128)(2,1)S(1)}, bf16[264,512]{1,0:T(8,128)(2,1)S(1)}, u32[]{:S(2)}, u32[]{:S(2)}) collective-permute-start(bf16[264,512]{1,0:T(8,128)(2,1)S(1)} %get-tuple-element.26.refs_0_), channel_id=1, source_target_pairs={{0,2},{1,3},{2,0},{3,1},{4,6},{5,7},{6,4},{7,5},{8,10},{9,11},{10,... | collective-permute-start | bytes 811016 | tf_op jit(solution)/shard_map/ppermute | solution.py:342
  3.5 23.2 %collective-permute-start.1 = (bf16[264,512]{1,0:T(8,128)(2,1)S(1)}, bf16[264,512]{1,0:T(8,128)(2,1)S(1)}, u32[]{:S(2)}, u32[]{:S(2)}) collective-permute-start(bf16[264,512]{1,0:T(8,128)(2,1)S(1)} %get-tuple-element.26.refs_0_), channel_id=1, source_target_pairs={{0,1},{1,0},{2,3},{3,2},{4,5},{5,4},{6,7},{7,6},{8,9},{9,8},{10,11... | collective-permute-start | bytes 811016 | tf_op jit(solution)/shard_map/ppermute | solution.py:342
  3.7 26.0 %collective-permute-start.3 = (bf16[256,384]{1,0:T(8,128)(2,1)S(1)}, bf16[256,384]{1,0:T(8,128)(2,1)S(1)}, u32[]{:S(2)}, u32[]{:S(2)}) collective-permute-start(bf16[256,384]{1,0:T(8,128)(2,1)S(1)} %get-tuple-element.28), channel_id=1, source_target_pairs={{0,3},{1,2},{2,1},{3,0},{4,7},{5,6},{6,5},{7,4},{8,11},{9,10},{10,... | collective-permute-start | bytes 589832 | tf_op jit(solution)/shard_map/ppermute | solution.py:342
  3.9 29.3 %copy-start.1 = (f32[256]{0:T(256)S(1)}, f32[256]{0:T(256)}, u32[]{:S(2)}) copy-start(f32[256]{0:T(256)} %param.10) | copy-start | bytes 3076
  3.9 35.1 %copy-start.2 = (f32[256]{0:T(256)S(1)}, f32[256]{0:T(256)}, u32[]{:S(2)}) copy-start(f32[256]{0:T(256)} %param.11) | copy-start | bytes 3076
  3.9 22.8 %collective-permute-start.2 = (bf16[264,128]{1,0:T(8,128)(2,1)S(1)}, bf16[264,128]{1,0:T(8,128)(2,1)S(1)}, u32[]{:S(2)}, u32[]{:S(2)}) collective-permute-start(bf16[264,128]{1,0:T(8,128)(2,1)S(1)} %get-tuple-element.27), channel_id=1, source_target_pairs={{0,3},{1,2},{2,1},{3,0},{4,7},{5,6},{6,5},{7,4},{8,11},{9,10},{10,... | collective-permute-start | bytes 202760 | tf_op jit(solution)/shard_map/ppermute | solution.py:342
  27.9 5.1 %collective-permute-start.4 = (f32[64,256]{1,0:T(8,128)S(1)}, f32[64,256]{1,0:T(8,128)S(1)}, u32[]{:S(2)}, u32[]{:S(2)}) collective-permute-start(f32[64,256]{1,0:T(8,128)S(1)} %get-tuple-element.29), channel_id=1, source_target_pairs={{0,4},{8,12},{16,20},{24,28},{4,0},{12,8},{20,16},{28,24},{1,5},{9... | collective-permute-start | bytes 196616 | tf_op jit(solution)/shard_map/ppermute | solution.py:337
  28.5 4.6 %collective-permute-start.5 = (f32[64,256]{1,0:T(8,128)S(1)}, f32[64,256]{1,0:T(8,128)S(1)}, u32[]{:S(2)}, u32[]{:S(2)}) collective-permute-start(f32[64,256]{1,0:T(8,128)S(1)} %get-tuple-element.30), channel_id=1, source_target_pairs={{4,8},{12,16},{20,24},{28,0},{8,4},{16,12},{24,20},{0,28},{5,9},{1... | collective-permute-start | bytes 196616 | tf_op jit(solution)/shard_map/ppermute | solution.py:337
  33.3 3.5 %collective-permute-start.6 = (f32[1,512]{1,0:T(1,128)S(1)}, f32[1,512]{1,0:T(1,128)S(1)}, u32[]{:S(2)}, u32[]{:S(2)}) collective-permute-start(f32[1,512]{1,0:T(1,128)S(1)} %get-tuple-element.32.refs_2_), channel_id=1, source_target_pairs={{0,3},{1,2},{2,1},{3,0},{4,7},{5,6},{6,5},{7,4},{8,11},{9,10},{10,... | collective-permute-start | bytes 6152 | tf_op jit(solution)/shard_map/ppermute | solution.py:342
  35.6 3.3 %collective-permute-start.7 = (f32[1,512]{1,0:T(1,128)S(1)}, f32[1,512]{1,0:T(1,128)S(1)}, u32[]{:S(2)}, u32[]{:S(2)}) collective-permute-start(f32[1,512]{1,0:T(1,128)S(1)} %get-tuple-element.32.refs_2_), channel_id=1, source_target_pairs={{0,2},{1,3},{2,0},{3,1},{4,6},{5,7},{6,4},{7,5},{8,10},{9,11},{10,... | collective-permute-start | bytes 6152 | tf_op jit(solution)/shard_map/ppermute | solution.py:342
  35.6 3.3 %collective-permute-start.8 = (f32[1,512]{1,0:T(1,128)S(1)}, f32[1,512]{1,0:T(1,128)S(1)}, u32[]{:S(2)}, u32[]{:S(2)}) collective-permute-start(f32[1,512]{1,0:T(1,128)S(1)} %get-tuple-element.32.refs_2_), channel_id=1, source_target_pairs={{0,1},{1,0},{2,3},{3,2},{4,5},{5,4},{6,7},{7,6},{8,9},{9,8},{10,11... | collective-permute-start | bytes 6152 | tf_op jit(solution)/shard_map/ppermute | solution.py:342
  39.3 14.2 %collective-permute-start.12 = (bf16[512,256]{1,0:T(8,128)(2,1)S(1)}, bf16[512,256]{1,0:T(8,128)(2,1)S(1)}, u32[]{:S(2)}, u32[]{:S(2)}) collective-permute-start(bf16[512,256]{1,0:T(8,128)(2,1)S(1)} %get-tuple-element.35.refs_0_), channel_id=1, source_target_pairs={{0,2},{1,3},{2,0},{3,1},{4,6},{5,7},{6,4},{7,5},{8,10},{9,11},{10,... | collective-permute-start | bytes 786440 | tf_op jit(solution)/shard_map/ppermute | solution.py:342
  41.1 13.5 %collective-permute-start.11 = (bf16[512,256]{1,0:T(8,128)(2,1)S(1)}, bf16[512,256]{1,0:T(8,128)(2,1)S(1)}, u32[]{:S(2)}, u32[]{:S(2)}) collective-permute-start(bf16[512,256]{1,0:T(8,128)(2,1)S(1)} %get-tuple-element.35.refs_0_), channel_id=1, source_target_pairs={{0,1},{1,0},{2,3},{3,2},{4,5},{5,4},{6,7},{7,6},{8,9},{9,8},{10,11... | collective-permute-start | bytes 786440 | tf_op jit(solution)/shard_map/ppermute | solution.py:342
  41.1 25.6 %collective-permute-start.10 = (bf16[384,256]{1,0:T(8,128)(2,1)S(1)}, bf16[384,256]{1,0:T(8,128)(2,1)S(1)}, u32[]{:S(2)}, u32[]{:S(2)}) collective-permute-start(bf16[384,256]{1,0:T(8,128)(2,1)S(1)} %get-tuple-element.34), channel_id=1, source_target_pairs={{0,3},{1,2},{2,1},{3,0},{4,7},{5,6},{6,5},{7,4},{8,11},{9,10},{10,... | collective-permute-start | bytes 589832 | tf_op jit(solution)/shard_map/ppermute | solution.py:342
  42.0 22.3 %collective-permute-start.9 = (bf16[128,256]{1,0:T(8,128)(2,1)S(1)}, bf16[128,256]{1,0:T(8,128)(2,1)S(1)}, u32[]{:S(2)}, u32[]{:S(2)}) collective-permute-start(bf16[128,256]{1,0:T(8,128)(2,1)S(1)} %get-tuple-element.33), channel_id=1, source_target_pairs={{0,3},{1,2},{2,1},{3,0},{4,7},{5,6},{6,5},{7,4},{8,11},{9,10},{10,... | collective-permute-start | bytes 196616 | tf_op jit(solution)/shard_map/ppermute | solution.py:342
  44.9 25.4 %copy-start = (bf16[256,1,512]{2,0,1:T(8,128)(2,1)S(1)}, bf16[256,1,512]{2,0,1:T(8,128)(2,1)}, u32[]{:S(2)}) copy-start(bf16[256,1,512]{2,0,1:T(8,128)(2,1)} %param.7) | copy-start | bytes 786436
  45.0 25.4 %copy-start.3 = (f32[256]{0:T(256)S(1)}, f32[256]{0:T(256)}, u32[]{:S(2)}) copy-start(f32[256]{0:T(256)} %param.13) | copy-start | bytes 3076
  64.6 2.9 %collective-permute-start.13 = (f32[64,256]{1,0:T(8,128)S(1)}, f32[64,256]{1,0:T(8,128)S(1)}, u32[]{:S(2)}, u32[]{:S(2)}) collective-permute-start(f32[64,256]{1,0:T(8,128)S(1)} %get-tuple-element.45), channel_id=1, source_target_pairs={{0,4},{8,12},{16,20},{24,28},{4,0},{12,8},{20,16},{28,24},{1,5},{9... | collective-permute-start | bytes 196616 | tf_op jit(solution)/shard_map/ppermute | solution.py:337
  65.7 4.6 %collective-permute-start.14 = (f32[64,256]{1,0:T(8,128)S(1)}, f32[64,256]{1,0:T(8,128)S(1)}, u32[]{:S(2)}, u32[]{:S(2)}) collective-permute-start(f32[64,256]{1,0:T(8,128)S(1)} %get-tuple-element.46), channel_id=1, source_target_pairs={{4,8},{12,16},{20,24},{28,0},{8,4},{16,12},{24,20},{0,28},{5,9},{1... | collective-permute-start | bytes 196616 | tf_op jit(solution)/shard_map/ppermute | solution.py:337
where the time goes:
time: 71.4 us; the launch traced here: 71.2 us
  waiting for transfers between devices  40.2 us (56%)
  Pallas kernels  16.3 us (23%)
  starting transfers between devices  14.6 us (20%)
    ppermute x11, waiting for transfers between devices, swap(): lax.ppermute(value, 'chan', [(i, i ^ step) for i in range(lax.axis_size('...  37.4 us
    ppermute x11, starting transfers between devices, swap(): lax.ppermute(value, 'chan', [(i, i ^ step) for i in range(lax.axis_size('...  10.8 us
    pallas_call x2, Pallas kernels, fetch(): pl.pallas_call(lambda *refs: fetch_kernel(weights.shape[0] - 1, *refs), o...  4.76 us
    ppermute x4, starting transfers between devices, with_row_neighbours(): lax.ppermute(send, 'rows', pairs + [(b, a) for a, b in pairs])  3.8 us
    pallas_call x1, Pallas kernels, first_main(): pl.pallas_call(lambda *refs: first_kernel(total, *refs), out_shape=jax.Sh...  3.4 us
    pallas_call x3, Pallas kernels, second_part(): pl.pallas_call(lambda *refs: part_kernel(k, *refs), out_shape=[jax.ShapeD...  3.12 us
    ppermute x4, waiting for transfers between devices, with_row_neighbours(): lax.ppermute(send, 'rows', pairs + [(b, a) for a, b in pairs])  2.78 us
  transfers between devices with their start and end apart: 15, of which 5 were waited for; matrix products, arithmetic and copies ran while one was open for 0% of the time, Pallas kernels for 19%

commit v1 on v0

--- a/solution.py
+++ b/solution.py
@@ -109,20 +109,31 @@
     return above, matmul(low, [taps[s, :, lanes] for s in range(3)])
 
 
-def gain_rows(parts, lanes, rows):
-    width = parts[0].shape[1]
-    step = min(width, lanes)
-    pieces = [part[:, k : k + step] for part in parts for k in range(0, width, step)]
-    result = jnp.concatenate([*pieces, jnp.zeros((rows - len(pieces), step), jnp.float32)], axis=0)
-    if lanes > step:
-        result = jnp.concatenate([result, jnp.zeros((rows, lanes - step), jnp.float32)], axis=1)
-    return result
-
-
-def gain_from(note, width):
+def thirds(value):
+    parts = []
+    for _ in range(3):
+        parts.append(value.astype(jnp.bfloat16).astype(jnp.float32))
+        value = value - parts[-1]
+    return parts
+
+
+def note_rows(values, lanes, rows):
+    pieces = []
+    for value in values:
+        step = min(value.shape[1], lanes)
+        for part in thirds(value):
+            for k in range(0, value.shape[1], step):
+                piece = part[:, k : k + step]
+                if lanes > step:
+                    piece = jnp.concatenate([piece, jnp.zeros((1, lanes - step), jnp.float32)], axis=1)
+                pieces.append(piece)
+    return jnp.concatenate([*pieces, jnp.zeros((rows - len(pieces), lanes), jnp.float32)], axis=0)
+
+
+def noted(note, width, skip=0):
     step = min(width, note.shape[1])
     count = width // step
-    rows = [note[k : k + 1, :step].astype(jnp.float32) for k in range(3 * count)]
+    rows = [note[skip + k : skip + k + 1, :step].astype(jnp.float32) for k in range(3 * count)]
     parts = [jnp.concatenate(rows[k * count : (k + 1) * count], axis=1) for k in range(3)]
     return (parts[0] + parts[1]) + parts[2]
 
@@ -136,13 +147,11 @@
     for copy in copies:
         copy.start()
     copies[1].wait()
-    parts, rest = [], gain[...]
-    for _ in range(3):
-        parts.append(rest.astype(jnp.bfloat16).astype(jnp.float32))
-        rest = rest - parts[-1]
-    for out in (whole, edge):
-        out[width:] = gain_rows(parts, out.shape[1], out.shape[0] - width).astype(out.dtype)
+    whole[width:] = note_rows([gain[...]], cells, whole.shape[0] - width).astype(whole.dtype)
     copies[0].wait()
+    values = whole[:width].astype(jnp.float32)
+    notes = [gain[...], jnp.sum(values * values, axis=0, keepdims=True)]
+    edge[width:] = note_rows(notes, edge.shape[1], edge.shape[0] - width).astype(edge.dtype)
     edge[:width] = edges_in(whole[:width])
     body[...] = whole[:width, WIDTH : cells - WIDTH]
 
@@ -154,7 +163,7 @@
 
 def to_send(block, gain):
     width, cells = block.shape
-    pieces = 3 * pl.cdiv(width, 2 * WIDTH)
+    pieces = 3 * (pl.cdiv(width, 2 * WIDTH) + cells // (2 * WIDTH))
     shapes = [(width + 8, cells), (width + 8 * pl.cdiv(pieces, 8), 2 * WIDTH), (width, cells - 2 * WIDTH)]
     return pl.pallas_call(
         send_kernel,
@@ -174,7 +183,7 @@
 
 
 def first_gains(wholes, edge, width):
-    return [gain_from(ref[width:], width) for ref in (*wholes, edge)]
+    return [noted(ref[width:], width) for ref in (*wholes, edge)]
 
 
 def first_edge_kernel(total, *refs):
@@ -197,33 +206,56 @@
     )(*wholes, edge, taps)
 
 
-def first_kernel(total, *refs):
-    wholes, (edge, body, taps, out, blocks, acts) = refs[:-6], refs[-6:]
-    width = wholes[0].shape[0] - 8
-    ends = edge[:width]
-    last = jnp.concatenate([ends[:, :WIDTH], body[...], ends[:, WIDTH:]], axis=1)
-    values = [ref[:width] for ref in wholes] + [last]
-    for k, block in enumerate(normed(values, first_gains(wholes, edge, width), total)):
-        blocks[k] = block
-    for k in range(len(values)):
-        part = main_taps(blocks[k], taps, owner_of(k), acts.at[k % 2])
+def first_upper_kernel(total, *refs):
+    wholes, (edge, taps, out, squares, acts) = refs[:-5], refs[-5:]
+    width, cells = wholes[0].shape[0] - 8, wholes[0].shape[1]
+    values = [ref[:width].astype(jnp.float32) for ref in wholes]
+    sums = noted(edge[width:], cells, 3 * pl.cdiv(width, edge.shape[1]))
+    sums = sum(jnp.sum(value * value, axis=0, keepdims=True) for value in values) + sums
+    squares[...] = sums
+    inverse = column_of(1.0 / jnp.sqrt(sums / total + 1e-6))
+    for k, value in enumerate(values):
+        block = silu(value.T * noted(wholes[k][width:], width) * inverse).astype(jnp.bfloat16)
+        part = main_taps(block, taps, owner_of(k), acts.at[k % 2])
         out[...] = part if k == 0 else out[...] + part
 
 
-def first_main(wholes, edge, body, taps):
+def first_upper(wholes, edge, taps):
     outs, total = taps.shape[1:]
     width, cells = wholes[0].shape[0] - 8, wholes[0].shape[1]
     return pl.pallas_call(
-        lambda *refs: first_kernel(total, *refs),
-        out_shape=jax.ShapeDtypeStruct((cells, outs), jnp.float32),
-        in_specs=[VMEM] * (len(wholes) + 3),
+        lambda *refs: first_upper_kernel(total, *refs),
+        out_shape=[
+            jax.ShapeDtypeStruct((cells, outs), jnp.float32),
+            jax.ShapeDtypeStruct((1, cells), jnp.float32),
+        ],
+        in_specs=[VMEM] * (len(wholes) + 2),
+        out_specs=[VMEM] * 2,
+        scratch_shapes=[pltpu.VMEM((2, 3, cells + 2 * WIDTH, width), jnp.bfloat16)],
+        compiler_params=PARAMS,
+    )(*wholes, edge, taps)
+
+
+def first_main_kernel(k, total, edge, body, taps, squares, before, out, acts):
+    width = body.shape[0]
+    ends = edge[:width]
+    last = jnp.concatenate([ends[:, :WIDTH], body[...], ends[:, WIDTH:]], axis=1).astype(jnp.float32)
+    inverse = column_of(1.0 / jnp.sqrt(squares[...] / total + 1e-6))
+    block = silu(last.T * noted(edge[width:], width) * inverse).astype(jnp.bfloat16)
+    out[...] = before[...] + main_taps(block, taps, owner_of(k), acts)
+
+
+def first_main(k, edge, body, taps, squares, before):
+    total = taps.shape[2]
+    return pl.pallas_call(
+        lambda *refs: first_main_kernel(k, total, *refs),
+        out_shape=jax.ShapeDtypeStruct(before.shape, before.dtype),
+        in_specs=[VMEM] * 5,
         out_specs=VMEM,
-        scratch_shapes=[
-            pltpu.VMEM((len(wholes) + 1, cells, width), jnp.bfloat16),
-            pltpu.VMEM((2, 3, cells + 2 * WIDTH, width), jnp.bfloat16),
-        ],
-        compiler_params=PARAMS,
-    )(*wholes, edge, body, taps)
+        input_output_aliases={4: 0},
+        scratch_shapes=[pltpu.VMEM((3, before.shape[0] + 2 * WIDTH, body.shape[0]), jnp.bfloat16)],
+        compiler_params=PARAMS,
+    )(edge, body, taps, squares, before)
 
 
 def part_kernel(k, block, taps, *refs):
@@ -359,7 +391,8 @@
     blocks, edge, body = gathered(*to_send(source, gain_first.reshape(1, -1)))
     sends = first_edge(blocks, edge, taps)
     edges = with_row_neighbours(sends)
-    main = first_main(blocks, edge, body, taps)
+    main, squares = first_upper(blocks, edge, taps)
+    main = first_main(count - 1, edge, body, taps, squares, main)
     middle, squares = pl.pallas_call(
         middle_kernel,
         out_shape=[

time: 71.4 us -> 72 us (level)
    pallas_call x1 -> x2, Pallas kernels: 3.4 us -> 3.86 us  [the longest x1 2.71 us: first_upper(): pl.pallas_call(lambda *refs: first_upper_kernel(total, *refs), out_shape=...]
  transfers between devices with their start and end apart: 15 -> 15, of which waited for: 5 -> 5; matrix products, arithmetic and copies ran while one was open for 0% -> 0% of each run, Pallas kernels for 19% -> 20%
where the time goes in v1:
time: 72 us; the launch traced here: 71.8 us
  waiting for transfers between devices  40.4 us (56%)
  Pallas kernels  16.7 us (23%)
  starting transfers between devices  14.5 us (20%)
    ppermute x11, waiting for transfers between devices, swap(): lax.ppermute(value, 'chan', [(i, i ^ step) for i in range(lax.axis_size('...  37.5 us
    ppermute x11, starting transfers between devices, swap(): lax.ppermute(value, 'chan', [(i, i ^ step) for i in range(lax.axis_size('...  10.8 us
    pallas_call x2, Pallas kernels, fetch(): pl.pallas_call(lambda *refs: fetch_kernel(weights.shape[0] - 1, *refs), o...  4.76 us
    ppermute x4, starting transfers between devices, with_row_neighbours(): lax.ppermute(send, 'rows', pairs + [(b, a) for a, b in pairs])  3.7 us
    pallas_call x3, Pallas kernels, second_part(): pl.pallas_call(lambda *refs: part_kernel(k, *refs), out_shape=[jax.ShapeD...  3.14 us
    ppermute x4, waiting for transfers between devices, with_row_neighbours(): lax.ppermute(send, 'rows', pairs + [(b, a) for a, b in pairs])  2.88 us
    pallas_call x1, Pallas kernels, first_upper(): pl.pallas_call(lambda *refs: first_upper_kernel(total, *refs), out_shape=...  2.71 us
  transfers between devices with their start and end apart: 15, of which 5 were waited for; matrix products, arithmetic and copies ran while one was open for 0% of the time, Pallas kernels for 20%

profile of v1, /device:TPU:9, one launch (start us, length us, event | category | flops | bytes accessed | tf_op | source)
XLA Modules:
  0.0 71.8 jit_solution(11880821883580343111)
XLA Ops:
  0.0 1.1 %shard_map.73 = (bf16[264,512]{1,0:T(8,128)(2,1)S(1)}, bf16[280,128]{1,0:T(8,128)(2,1)S(1)}, bf16[256,384]{1,0:T(8,128)(2,1)S(1)}) custom-call(bf16[256,512]{1,0:T(8,128)(2,1)} %bitcast.6, f32[1,256]{1,0:T(1,128)} %bitcast.11), custom_call_target="tpu_custom_call" | custom-call | tf_op jit(solution)/shard_map/pallas_call | solution.py:168
  1.1 2.4 %collective-permute-start.2 = (bf16[264,512]{1,0:T(8,128)(2,1)S(1)}, bf16[264,512]{1,0:T(8,128)(2,1)S(1)}, u32[]{:S(2)}, u32[]{:S(2)}) collective-permute-start(bf16[264,512]{1,0:T(8,128)(2,1)S(1)} %get-tuple-element.30.refs_0_), channel_id=1, source_target_pairs={{0,2},{1,3},{2,0},{3,1},{4,6},{5,7},{6,4},{7,5},{8,10},{9,11},{10,... | collective-permute-start | bytes 811016 | tf_op jit(solution)/shard_map/ppermute | solution.py:374
  3.5 0.2 collective-permute-start.3
  3.7 0.2 collective-permute-start.1
  3.9 1.3 %collective-permute-start = (bf16[280,128]{1,0:T(8,128)(2,1)S(1)}, bf16[280,128]{1,0:T(8,128)(2,1)S(1)}, u32[]{:S(2)}, u32[]{:S(2)}) collective-permute-start(bf16[280,128]{1,0:T(8,128)(2,1)S(1)} %get-tuple-element.28), channel_id=1, source_target_pairs={{0,3},{1,2},{2,1},{3,0},{4,7},{5,6},{6,5},{7,4},{8,11},{9,10},{10,... | collective-permute-start | bytes 215048 | tf_op jit(solution)/shard_map/ppermute | solution.py:374
  5.1 2.4 %shard_map.74.refs_4_.refs_2_ = bf16[9,256,1024]{2,1,0:T(8,128)(2,1)S(1)} custom-call(bf16[3,3,3,256,1024]{4,3,2,1,0:T(8,128)(2,1)} %refs_0_.2), custom_call_target="tpu_custom_call" | custom-call | tf_op jit(solution)/shard_map/pallas_call | solution.py:53
  7.5 19.4 %collective-permute-done.refs_3_.refs_0_ = bf16[280,128]{1,0:T(8,128)(2,1)S(1)} collective-permute-done((bf16[280,128]{1,0:T(8,128)(2,1)S(1)}, bf16[280,128]{1,0:T(8,128)(2,1)S(1)}, u32[]{:S(2)}, u32[]{:S(2)}) %collective-permute-start) | collective-permute-done | bytes 71712 | tf_op jit(solution)/shard_map/ppermute | solution.py:374
  26.9 0.0 collective-permute-done.2.refs_1_
  26.9 0.0 collective-permute-done.3.refs_2_
  26.9 1.2 %shard_map.77 = (f32[64,256]{1,0:T(8,128)S(1)}, f32[64,256]{1,0:T(8,128)S(1)}) custom-call(bf16[264,512]{1,0:T(8,128)(2,1)S(1)} %get-tuple-element.30.refs_0_, bf16[264,512]{1,0:T(8,128)(2,1)S(1)} %collective-permute-done.2.refs_1_, bf16[264,512]{1,0:T(8,128)(2,1)S(1)} %collective-permute-done.3.refs_2_, ...), custom_call_target="tpu_custom_call" | custom-call | tf_op jit(solution)/shard_map/pallas_call | solution.py:200
  28.1 0.6 collective-permute-start.4
  28.7 1.2 %collective-permute-start.5 = (f32[64,256]{1,0:T(8,128)S(1)}, f32[64,256]{1,0:T(8,128)S(1)}, u32[]{:S(2)}, u32[]{:S(2)}) collective-permute-start(f32[64,256]{1,0:T(8,128)S(1)} %get-tuple-element.34), channel_id=1, source_target_pairs={{4,8},{12,16},{20,24},{28,0},{8,4},{16,12},{24,20},{0,28},{5,9},{1... | collective-permute-start | bytes 196616 | tf_op jit(solution)/shard_map/ppermute | solution.py:369
  29.8 2.7 %shard_map.75 = (f32[512,256]{1,0:T(8,128)S(1)}, f32[1,512]{1,0:T(1,128)S(1)}) custom-call(bf16[264,512]{1,0:T(8,128)(2,1)S(1)} %get-tuple-element.30.refs_0_, bf16[264,512]{1,0:T(8,128)(2,1)S(1)} %collective-permute-done.2.refs_1_, bf16[264,512]{1,0:T(8,128)(2,1)S(1)} %collective-permute-done.3.refs_2_, ...), custom_call_target="tpu_custom_call" | custom-call | tf_op jit(solution)/shard_map/pallas_call | solution.py:226
  32.6 0.0 collective-permute-done.1.refs_1_
  32.6 1.1 %shard_map.76.main = f32[512,256]{1,0:T(8,128)S(1)} custom-call(bf16[280,128]{1,0:T(8,128)(2,1)S(1)} %collective-permute-done.refs_3_.refs_0_, bf16[256,384]{1,0:T(8,128)(2,1)S(1)} %collective-permute-done.1.refs_1_, bf16[9,256,1024]{2,1,0:T(8,128)(2,1)S(1)} %shard_map.74.refs_4_.refs_2_, ...), custom_call_target="tpu_custom_call", output_to_operand_aliasing={{}: (4, {})} | custom-call | tf_op jit(solution)/shard_map/pallas_call | solution.py:250
  33.7 0.0 collective-permute-done.4.first
  33.7 0.0 collective-permute-done.5.second
  33.7 0.0 copy-done.1
  33.7 0.2 shard_map.78
  33.9 2.2 %collective-permute-start.6 = (f32[1,512]{1,0:T(1,128)S(1)}, f32[1,512]{1,0:T(1,128)S(1)}, u32[]{:S(2)}, u32[]{:S(2)}) collective-permute-start(f32[1,512]{1,0:T(1,128)S(1)} %get-tuple-element.36.refs_2_), channel_id=1, source_target_pairs={{0,3},{1,2},{2,1},{3,0},{4,7},{5,6},{6,5},{7,4},{8,11},{9,10},{10,... | collective-permute-start | bytes 6152 | tf_op jit(solution)/shard_map/ppermute | solution.py:374
  36.2 0.0 collective-permute-start.7
  36.2 1.3 %collective-permute-start.8 = (f32[1,512]{1,0:T(1,128)S(1)}, f32[1,512]{1,0:T(1,128)S(1)}, u32[]{:S(2)}, u32[]{:S(2)}) collective-permute-start(f32[1,512]{1,0:T(1,128)S(1)} %get-tuple-element.36.refs_2_), channel_id=1, source_target_pairs={{0,1},{1,0},{2,3},{3,2},{4,5},{5,4},{6,7},{7,6},{8,9},{9,8},{10,11... | collective-permute-start | bytes 6152 | tf_op jit(solution)/shard_map/ppermute | solution.py:374
  37.4 0.0 collective-permute-done.6.refs_3_
  37.5 2.1 %collective-permute-done.7.refs_4_ = f32[1,512]{1,0:T(1,128)S(1)} collective-permute-done((f32[1,512]{1,0:T(1,128)S(1)}, f32[1,512]{1,0:T(1,128)S(1)}, u32[]{:S(2)}, u32[]{:S(2)}) %collective-permute-start.7) | collective-permute-done | bytes 2080 | tf_op jit(solution)/shard_map/ppermute | solution.py:374
  39.5 0.0 collective-permute-done.8.refs_5_
  39.5 0.3 shard_map.79
  39.9 1.8 %collective-permute-start.12 = (bf16[512,256]{1,0:T(8,128)(2,1)S(1)}, bf16[512,256]{1,0:T(8,128)(2,1)S(1)}, u32[]{:S(2)}, u32[]{:S(2)}) collective-permute-start(bf16[512,256]{1,0:T(8,128)(2,1)S(1)} %get-tuple-element.39.refs_0_), channel_id=1, source_target_pairs={{0,2},{1,3},{2,0},{3,1},{4,6},{5,7},{6,4},{7,5},{8,10},{9,11},{10,... | collective-permute-start | bytes 786440 | tf_op jit(solution)/shard_map/ppermute | solution.py:374
  41.7 0.0 collective-permute-start.11
  41.7 0.9 %collective-permute-start.10 = (bf16[384,256]{1,0:T(8,128)(2,1)S(1)}, bf16[384,256]{1,0:T(8,128)(2,1)S(1)}, u32[]{:S(2)}, u32[]{:S(2)}) collective-permute-start(bf16[384,256]{1,0:T(8,128)(2,1)S(1)} %get-tuple-element.38), channel_id=1, source_target_pairs={{0,3},{1,2},{2,1},{3,0},{4,7},{5,6},{6,5},{7,4},{8,11},{9,10},{10,... | collective-permute-start | bytes 589832 | tf_op jit(solution)/shard_map/ppermute | solution.py:374
  42.6 0.6 collective-permute-start.9
  43.2 2.4 %shard_map.80.refs_1_.refs_2_ = bf16[9,256,1024]{2,1,0:T(8,128)(2,1)S(1)} custom-call(bf16[3,3,3,256,1024]{4,3,2,1,0:T(8,128)(2,1)} %refs_0_.3), custom_call_target="tpu_custom_call" | custom-call | tf_op jit(solution)/shard_map/pallas_call | solution.py:53
  45.5 0.0 copy-start
  45.6 0.0 copy-start.3
  45.6 1.0 %shard_map.81 = (f32[512,256]{1,0:T(8,128)S(1)}, f32[64,256]{1,0:T(8,128)S(1)}, f32[64,256]{1,0:T(8,128)S(1)}) custom-call(bf16[512,256]{1,0:T(8,128)(2,1)S(1)} %get-tuple-element.39.refs_0_, bf16[9,256,1024]{2,1,0:T(8,128)(2,1)S(1)} %shard_map.80.refs_1_.refs_2_), custom_call_target="tpu_custom_call" | custom-call | tf_op jit(solution)/shard_map/pallas_call | solution.py:271
  46.6 7.5 %collective-permute-done.12.refs_0_ = bf16[512,256]{1,0:T(8,128)(2,1)S(1)} collective-permute-done((bf16[512,256]{1,0:T(8,128)(2,1)S(1)}, bf16[512,256]{1,0:T(8,128)(2,1)S(1)}, u32[]{:S(2)}, u32[]{:S(2)}) %collective-permute-start.12) | collective-permute-done | bytes 262176 | tf_op jit(solution)/shard_map/ppermute | solution.py:374
  54.1 1.0 %shard_map.82 = (f32[512,256]{1,0:T(8,128)S(1)}, f32[64,256]{1,0:T(8,128)S(1)}, f32[64,256]{1,0:T(8,128)S(1)}) custom-call(bf16[512,256]{1,0:T(8,128)(2,1)S(1)} %collective-permute-done.12.refs_0_, bf16[9,256,1024]{2,1,0:T(8,128)(2,1)S(1)} %shard_map.80.refs_1_.refs_2_, ...), custom_call_target="tpu_custom_call", output_to_operand_aliasing={{0}: (2, {}), {1}: (3, {}), {2}: (4, {})} | custom-call | tf_op jit(solution)/shard_map/pallas_call | solution.py:271
  55.1 0.0 collective-permute-done.11.refs_0_
  55.2 1.1 %shard_map.83 = (f32[512,256]{1,0:T(8,128)S(1)}, f32[64,256]{1,0:T(8,128)S(1)}, f32[64,256]{1,0:T(8,128)S(1)}) custom-call(bf16[512,256]{1,0:T(8,128)(2,1)S(1)} %collective-permute-done.11.refs_0_, bf16[9,256,1024]{2,1,0:T(8,128)(2,1)S(1)} %shard_map.80.refs_1_.refs_2_, ...), custom_call_target="tpu_custom_call", output_to_operand_aliasing={{0}: (2, {}), {1}: (3, {}), {2}: (4, {})} | custom-call | tf_op jit(solution)/shard_map/pallas_call | solution.py:271
  56.2 8.6 %collective-permute-done.9.refs_0_ = bf16[128,256]{1,0:T(8,128)(2,1)S(1)} collective-permute-done((bf16[128,256]{1,0:T(8,128)(2,1)S(1)}, bf16[128,256]{1,0:T(8,128)(2,1)S(1)}, u32[]{:S(2)}, u32[]{:S(2)}) %collective-permute-start.9) | collective-permute-done | bytes 65568 | tf_op jit(solution)/shard_map/ppermute | solution.py:374
  64.8 0.4 shard_map.85
  65.2 1.1 %collective-permute-start.13 = (f32[64,256]{1,0:T(8,128)S(1)}, f32[64,256]{1,0:T(8,128)S(1)}, u32[]{:S(2)}, u32[]{:S(2)}) collective-permute-start(f32[64,256]{1,0:T(8,128)S(1)} %get-tuple-element.49), channel_id=1, source_target_pairs={{0,4},{8,12},{16,20},{24,28},{4,0},{12,8},{20,16},{28,24},{1,5},{9... | collective-permute-start | bytes 196616 | tf_op jit(solution)/shard_map/ppermute | solution.py:369
  66.3 0.9 %collective-permute-start.14 = (f32[64,256]{1,0:T(8,128)S(1)}, f32[64,256]{1,0:T(8,128)S(1)}, u32[]{:S(2)}, u32[]{:S(2)}) collective-permute-start(f32[64,256]{1,0:T(8,128)S(1)} %get-tuple-element.50), channel_id=1, source_target_pairs={{4,8},{12,16},{20,24},{28,0},{8,4},{16,12},{24,20},{0,28},{5,9},{1... | collective-permute-start | bytes 196616 | tf_op jit(solution)/shard_map/ppermute | solution.py:369
  67.2 0.0 collective-permute-done.10.refs_1_
  67.2 0.8 %shard_map.84.main = f32[512,256]{1,0:T(8,128)S(1)} custom-call(bf16[128,256]{1,0:T(8,128)(2,1)S(1)} %collective-permute-done.9.refs_0_, bf16[384,256]{1,0:T(8,128)(2,1)S(1)} %collective-permute-done.10.refs_1_, bf16[9,256,1024]{2,1,0:T(8,128)(2,1)S(1)} %shard_map.80.refs_1_.refs_2_, ...), custom_call_target="tpu_custom_call", output_to_operand_aliasing={{}: (3, {})} | custom-call | tf_op jit(solution)/shard_map/pallas_call | solution.py:303
  68.0 0.0 collective-permute-done.13.first
  68.0 2.9 %collective-permute-done.14.second = f32[64,256]{1,0:T(8,128)S(1)} collective-permute-done((f32[64,256]{1,0:T(8,128)S(1)}, f32[64,256]{1,0:T(8,128)S(1)}, u32[]{:S(2)}, u32[]{:S(2)}) %collective-permute-start.14) | collective-permute-done | bytes 65568 | tf_op jit(solution)/shard_map/ppermute | solution.py:369
  70.9 0.0 copy-done
  70.9 0.9 %shard_map.86 = bf16[256,512]{1,0:T(8,128)(2,1)} custom-call(f32[512,256]{1,0:T(8,128)S(1)} %shard_map.84.main, f32[64,256]{1,0:T(8,128)S(1)} %collective-permute-done.13.first, f32[64,256]{1,0:T(8,128)S(1)} %collective-permute-done.14.second, f32[1,256]{1,0:T(1,128)S(1)} %bitcast.10, bf16[256,512]{1,0:T(8,128)(2,1)S(1)} %bitcast.7), custom_call_target="tpu_custom_call" | custom-call | tf_op jit(solution)/shard_map/pallas_call | solution.py:416
  (4 shorter events, 0.0 us)
Async XLA Ops:
  1.1 25.8 %collective-permute-start.2 = (bf16[264,512]{1,0:T(8,128)(2,1)S(1)}, bf16[264,512]{1,0:T(8,128)(2,1)S(1)}, u32[]{:S(2)}, u32[]{:S(2)}) collective-permute-start(bf16[264,512]{1,0:T(8,128)(2,1)S(1)} %get-tuple-element.30.refs_0_), channel_id=1, source_target_pairs={{0,2},{1,3},{2,0},{3,1},{4,6},{5,7},{6,4},{7,5},{8,10},{9,11},{10,... | collective-permute-start | bytes 811016 | tf_op jit(solution)/shard_map/ppermute | solution.py:374
  3.5 23.4 %collective-permute-start.3 = (bf16[264,512]{1,0:T(8,128)(2,1)S(1)}, bf16[264,512]{1,0:T(8,128)(2,1)S(1)}, u32[]{:S(2)}, u32[]{:S(2)}) collective-permute-start(bf16[264,512]{1,0:T(8,128)(2,1)S(1)} %get-tuple-element.30.refs_0_), channel_id=1, source_target_pairs={{0,1},{1,0},{2,3},{3,2},{4,5},{5,4},{6,7},{7,6},{8,9},{9,8},{10,11... | collective-permute-start | bytes 811016 | tf_op jit(solution)/shard_map/ppermute | solution.py:374
  3.7 28.9 %collective-permute-start.1 = (bf16[256,384]{1,0:T(8,128)(2,1)S(1)}, bf16[256,384]{1,0:T(8,128)(2,1)S(1)}, u32[]{:S(2)}, u32[]{:S(2)}) collective-permute-start(bf16[256,384]{1,0:T(8,128)(2,1)S(1)} %get-tuple-element.29), channel_id=1, source_target_pairs={{0,3},{1,2},{2,1},{3,0},{4,7},{5,6},{6,5},{7,4},{8,11},{9,10},{10,... | collective-permute-start | bytes 589832 | tf_op jit(solution)/shard_map/ppermute | solution.py:374
  3.9 29.9 %copy-start.1 = (f32[256]{0:T(256)S(1)}, f32[256]{0:T(256)}, u32[]{:S(2)}) copy-start(f32[256]{0:T(256)} %param.10) | copy-start | bytes 3076
  3.9 35.7 %copy-start.2 = (f32[256]{0:T(256)S(1)}, f32[256]{0:T(256)}, u32[]{:S(2)}) copy-start(f32[256]{0:T(256)} %param.11) | copy-start | bytes 3076
  3.9 23.0 %collective-permute-start = (bf16[280,128]{1,0:T(8,128)(2,1)S(1)}, bf16[280,128]{1,0:T(8,128)(2,1)S(1)}, u32[]{:S(2)}, u32[]{:S(2)}) collective-permute-start(bf16[280,128]{1,0:T(8,128)(2,1)S(1)} %get-tuple-element.28), channel_id=1, source_target_pairs={{0,3},{1,2},{2,1},{3,0},{4,7},{5,6},{6,5},{7,4},{8,11},{9,10},{10,... | collective-permute-start | bytes 215048 | tf_op jit(solution)/shard_map/ppermute | solution.py:374
  28.1 5.6 %collective-permute-start.4 = (f32[64,256]{1,0:T(8,128)S(1)}, f32[64,256]{1,0:T(8,128)S(1)}, u32[]{:S(2)}, u32[]{:S(2)}) collective-permute-start(f32[64,256]{1,0:T(8,128)S(1)} %get-tuple-element.33), channel_id=1, source_target_pairs={{0,4},{8,12},{16,20},{24,28},{4,0},{12,8},{20,16},{28,24},{1,5},{9... | collective-permute-start | bytes 196616 | tf_op jit(solution)/shard_map/ppermute | solution.py:369
  28.7 5.1 %collective-permute-start.5 = (f32[64,256]{1,0:T(8,128)S(1)}, f32[64,256]{1,0:T(8,128)S(1)}, u32[]{:S(2)}, u32[]{:S(2)}) collective-permute-start(f32[64,256]{1,0:T(8,128)S(1)} %get-tuple-element.34), channel_id=1, source_target_pairs={{4,8},{12,16},{20,24},{28,0},{8,4},{16,12},{24,20},{0,28},{5,9},{1... | collective-permute-start | bytes 196616 | tf_op jit(solution)/shard_map/ppermute | solution.py:369
  33.9 3.5 %collective-permute-start.6 = (f32[1,512]{1,0:T(1,128)S(1)}, f32[1,512]{1,0:T(1,128)S(1)}, u32[]{:S(2)}, u32[]{:S(2)}) collective-permute-start(f32[1,512]{1,0:T(1,128)S(1)} %get-tuple-element.36.refs_2_), channel_id=1, source_target_pairs={{0,3},{1,2},{2,1},{3,0},{4,7},{5,6},{6,5},{7,4},{8,11},{9,10},{10,... | collective-permute-start | bytes 6152 | tf_op jit(solution)/shard_map/ppermute | solution.py:374
  36.2 3.3 %collective-permute-start.7 = (f32[1,512]{1,0:T(1,128)S(1)}, f32[1,512]{1,0:T(1,128)S(1)}, u32[]{:S(2)}, u32[]{:S(2)}) collective-permute-start(f32[1,512]{1,0:T(1,128)S(1)} %get-tuple-element.36.refs_2_), channel_id=1, source_target_pairs={{0,2},{1,3},{2,0},{3,1},{4,6},{5,7},{6,4},{7,5},{8,10},{9,11},{10,... | collective-permute-start | bytes 6152 | tf_op jit(solution)/shard_map/ppermute | solution.py:374
  36.2 3.3 %collective-permute-start.8 = (f32[1,512]{1,0:T(1,128)S(1)}, f32[1,512]{1,0:T(1,128)S(1)}, u32[]{:S(2)}, u32[]{:S(2)}) collective-permute-start(f32[1,512]{1,0:T(1,128)S(1)} %get-tuple-element.36.refs_2_), channel_id=1, source_target_pairs={{0,1},{1,0},{2,3},{3,2},{4,5},{5,4},{6,7},{7,6},{8,9},{9,8},{10,11... | collective-permute-start | bytes 6152 | tf_op jit(solution)/shard_map/ppermute | solution.py:374
  39.9 14.2 %collective-permute-start.12 = (bf16[512,256]{1,0:T(8,128)(2,1)S(1)}, bf16[512,256]{1,0:T(8,128)(2,1)S(1)}, u32[]{:S(2)}, u32[]{:S(2)}) collective-permute-start(bf16[512,256]{1,0:T(8,128)(2,1)S(1)} %get-tuple-element.39.refs_0_), channel_id=1, source_target_pairs={{0,2},{1,3},{2,0},{3,1},{4,6},{5,7},{6,4},{7,5},{8,10},{9,11},{10,... | collective-permute-start | bytes 786440 | tf_op jit(solution)/shard_map/ppermute | solution.py:374
  41.7 13.5 %collective-permute-start.11 = (bf16[512,256]{1,0:T(8,128)(2,1)S(1)}, bf16[512,256]{1,0:T(8,128)(2,1)S(1)}, u32[]{:S(2)}, u32[]{:S(2)}) collective-permute-start(bf16[512,256]{1,0:T(8,128)(2,1)S(1)} %get-tuple-element.39.refs_0_), channel_id=1, source_target_pairs={{0,1},{1,0},{2,3},{3,2},{4,5},{5,4},{6,7},{7,6},{8,9},{9,8},{10,11... | collective-permute-start | bytes 786440 | tf_op jit(solution)/shard_map/ppermute | solution.py:374
  41.7 25.5 %collective-permute-start.10 = (bf16[384,256]{1,0:T(8,128)(2,1)S(1)}, bf16[384,256]{1,0:T(8,128)(2,1)S(1)}, u32[]{:S(2)}, u32[]{:S(2)}) collective-permute-start(bf16[384,256]{1,0:T(8,128)(2,1)S(1)} %get-tuple-element.38), channel_id=1, source_target_pairs={{0,3},{1,2},{2,1},{3,0},{4,7},{5,6},{6,5},{7,4},{8,11},{9,10},{10,... | collective-permute-start | bytes 589832 | tf_op jit(solution)/shard_map/ppermute | solution.py:374
  42.6 22.3 %collective-permute-start.9 = (bf16[128,256]{1,0:T(8,128)(2,1)S(1)}, bf16[128,256]{1,0:T(8,128)(2,1)S(1)}, u32[]{:S(2)}, u32[]{:S(2)}) collective-permute-start(bf16[128,256]{1,0:T(8,128)(2,1)S(1)} %get-tuple-element.37), channel_id=1, source_target_pairs={{0,3},{1,2},{2,1},{3,0},{4,7},{5,6},{6,5},{7,4},{8,11},{9,10},{10,... | collective-permute-start | bytes 196616 | tf_op jit(solution)/shard_map/ppermute | solution.py:374
  45.5 25.4 %copy-start = (bf16[256,1,512]{2,0,1:T(8,128)(2,1)S(1)}, bf16[256,1,512]{2,0,1:T(8,128)(2,1)}, u32[]{:S(2)}) copy-start(bf16[256,1,512]{2,0,1:T(8,128)(2,1)} %param.7) | copy-start | bytes 786436
  45.6 25.4 %copy-start.3 = (f32[256]{0:T(256)S(1)}, f32[256]{0:T(256)}, u32[]{:S(2)}) copy-start(f32[256]{0:T(256)} %param.13) | copy-start | bytes 3076
  65.2 2.8 %collective-permute-start.13 = (f32[64,256]{1,0:T(8,128)S(1)}, f32[64,256]{1,0:T(8,128)S(1)}, u32[]{:S(2)}, u32[]{:S(2)}) collective-permute-start(f32[64,256]{1,0:T(8,128)S(1)} %get-tuple-element.49), channel_id=1, source_target_pairs={{0,4},{8,12},{16,20},{24,28},{4,0},{12,8},{20,16},{28,24},{1,5},{9... | collective-permute-start | bytes 196616 | tf_op jit(solution)/shard_map/ppermute | solution.py:369
  66.3 4.6 %collective-permute-start.14 = (f32[64,256]{1,0:T(8,128)S(1)}, f32[64,256]{1,0:T(8,128)S(1)}, u32[]{:S(2)}, u32[]{:S(2)}) collective-permute-start(f32[64,256]{1,0:T(8,128)S(1)} %get-tuple-element.50), channel_id=1, source_target_pairs={{4,8},{12,16},{20,24},{28,0},{8,4},{16,12},{24,20},{0,28},{5,9},{1... | collective-permute-start | bytes 196616 | tf_op jit(solution)/shard_map/ppermute | solution.py:369

commit v2 on v1

--- a/solution.py
+++ b/solution.py
@@ -138,7 +138,7 @@
     return (parts[0] + parts[1]) + parts[2]
 
 
-def send_kernel(source, note, whole, edge, body, gain, sems):
+def send_kernel(source, note, whole, gain, sems):
     width, cells = source.shape
     copies = [
         pltpu.make_async_copy(source, whole.at[:width], sems.at[0]),
@@ -149,8 +149,12 @@
     copies[1].wait()
     whole[width:] = note_rows([gain[...]], cells, whole.shape[0] - width).astype(whole.dtype)
     copies[0].wait()
+
+
+def rest_kernel(whole, edge, body):
+    width, cells = body.shape[0], whole.shape[1]
     values = whole[:width].astype(jnp.float32)
-    notes = [gain[...], jnp.sum(values * values, axis=0, keepdims=True)]
+    notes = [noted(whole[width:], width), jnp.sum(values * values, axis=0, keepdims=True)]
     edge[width:] = note_rows(notes, edge.shape[1], edge.shape[0] - width).astype(edge.dtype)
     edge[:width] = edges_in(whole[:width])
     body[...] = whole[:width, WIDTH : cells - WIDTH]
@@ -163,16 +167,27 @@
 
 def to_send(block, gain):
     width, cells = block.shape
+    return pl.pallas_call(
+        send_kernel,
+        out_shape=pltpu.VMEM((width + 8, cells), block.dtype),
+        in_specs=[HBM] * 2,
+        out_specs=VMEM,
+        scratch_shapes=[pltpu.VMEM(gain.shape, gain.dtype), pltpu.SemaphoreType.DMA((2,))],
+        compiler_params=PARAMS,
+    )(*[pltpu.with_memory_space_constraint(value, pltpu.HBM) for value in (block, gain)])
+
+
+def rest_of(whole):
+    width, cells = whole.shape[0] - 8, whole.shape[1]
     pieces = 3 * (pl.cdiv(width, 2 * WIDTH) + cells // (2 * WIDTH))
-    shapes = [(width + 8, cells), (width + 8 * pl.cdiv(pieces, 8), 2 * WIDTH), (width, cells - 2 * WIDTH)]
-    return pl.pallas_call(
-        send_kernel,
-        out_shape=[pltpu.VMEM(shape, block.dtype) for shape in shapes],
-        in_specs=[HBM] * 2,
-        out_specs=[VMEM] * 3,
-        scratch_shapes=[pltpu.VMEM(gain.shape, gain.dtype), pltpu.SemaphoreType.DMA((2,))],
-        compiler_params=PARAMS,
-    )(*[pltpu.with_memory_space_constraint(value, pltpu.HBM) for value in (block, gain)])
+    shapes = [(width + 8 * pl.cdiv(pieces, 8), 2 * WIDTH), (width, cells - 2 * WIDTH)]
+    return pl.pallas_call(
+        rest_kernel,
+        out_shape=[pltpu.VMEM(shape, whole.dtype) for shape in shapes],
+        in_specs=[VMEM],
+        out_specs=[VMEM] * 2,
+        compiler_params=PARAMS,
+    )(whole)
 
 
 def normed(values, gains, total):
@@ -388,7 +403,8 @@
     count = lax.axis_size("chan")
     source = features.reshape(channels, cells)
     taps = fetch(weight_first)
-    blocks, edge, body = gathered(*to_send(source, gain_first.reshape(1, -1)))
+    whole = to_send(source, gain_first.reshape(1, -1))
+    blocks, edge, body = gathered(whole, *rest_of(whole))
     sends = first_edge(blocks, edge, taps)
     edges = with_row_neighbours(sends)
     main, squares = first_upper(blocks, edge, taps)

time: 72 us -> 71.9 us (level)
  no operation moved by 1% of the time
where the time goes in v2:
time: 71.9 us; the launch traced here: 71.7 us
  waiting for transfers between devices  40.2 us (56%)
  Pallas kernels  16.7 us (23%)
  starting transfers between devices  14.6 us (20%)
    ppermute x11, waiting for transfers between devices, swap(): lax.ppermute(value, 'chan', [(i, i ^ step) for i in range(lax.axis_size('...  37.3 us
    ppermute x11, starting transfers between devices, swap(): lax.ppermute(value, 'chan', [(i, i ^ step) for i in range(lax.axis_size('...  10.9 us
    pallas_call x2, Pallas kernels, fetch(): pl.pallas_call(lambda *refs: fetch_kernel(weights.shape[0] - 1, *refs), o...  4.76 us
    ppermute x4, starting transfers between devices, with_row_neighbours(): lax.ppermute(send, 'rows', pairs + [(b, a) for a, b in pairs])  3.7 us
    pallas_call x3, Pallas kernels, second_part(): pl.pallas_call(lambda *refs: part_kernel(k, *refs), out_shape=[jax.ShapeD...  3.14 us
    ppermute x4, waiting for transfers between devices, with_row_neighbours(): lax.ppermute(send, 'rows', pairs + [(b, a) for a, b in pairs])  2.87 us
    pallas_call x1, Pallas kernels, first_upper(): pl.pallas_call(lambda *refs: first_upper_kernel(total, *refs), out_shape=...  2.71 us
  transfers between devices with their start and end apart: 15, of which 5 were waited for; matrix products, arithmetic and copies ran while one was open for 0% of the time, Pallas kernels for 20%

profile of v2, /device:TPU:9, one launch (start us, length us, event | category | flops | bytes accessed | tf_op | source)
XLA Modules:
  0.0 71.7 jit_solution(2831001597171741753)
XLA Ops:
  0.0 1.0 %shard_map.73.whole.refs_0_ = bf16[264,512]{1,0:T(8,128)(2,1)S(1)} custom-call(bf16[256,512]{1,0:T(8,128)(2,1)} %bitcast.6, f32[1,256]{1,0:T(1,128)} %bitcast.11), custom_call_target="tpu_custom_call" | custom-call | tf_op jit(solution)/shard_map/pallas_call | solution.py:170
  1.0 2.4 %collective-permute-start.2 = (bf16[264,512]{1,0:T(8,128)(2,1)S(1)}, bf16[264,512]{1,0:T(8,128)(2,1)S(1)}, u32[]{:S(2)}, u32[]{:S(2)}) collective-permute-start(bf16[264,512]{1,0:T(8,128)(2,1)S(1)} %shard_map.73.whole.refs_0_), channel_id=1, source_target_pairs={{0,2},{1,3},{2,0},{3,1},{4,6},{5,7},{6,4},{7,5},{8,10},{9,11},{10,... | collective-permute-start | bytes 811016 | tf_op jit(solution)/shard_map/ppermute | solution.py:389
  3.3 0.2 collective-permute-start.3
  3.5 0.1 shard_map.74
  3.7 0.3 collective-permute-start.1
  3.9 1.3 %collective-permute-start = (bf16[280,128]{1,0:T(8,128)(2,1)S(1)}, bf16[280,128]{1,0:T(8,128)(2,1)S(1)}, u32[]{:S(2)}, u32[]{:S(2)}) collective-permute-start(bf16[280,128]{1,0:T(8,128)(2,1)S(1)} %get-tuple-element.27), channel_id=1, source_target_pairs={{0,3},{1,2},{2,1},{3,0},{4,7},{5,6},{6,5},{7,4},{8,11},{9,10},{10,... | collective-permute-start | bytes 215048 | tf_op jit(solution)/shard_map/ppermute | solution.py:389
  5.2 2.4 %shard_map.75.refs_4_.refs_2_ = bf16[9,256,1024]{2,1,0:T(8,128)(2,1)S(1)} custom-call(bf16[3,3,3,256,1024]{4,3,2,1,0:T(8,128)(2,1)} %refs_0_.2), custom_call_target="tpu_custom_call" | custom-call | tf_op jit(solution)/shard_map/pallas_call | solution.py:53
  7.6 19.1 %collective-permute-done.refs_3_.refs_0_ = bf16[280,128]{1,0:T(8,128)(2,1)S(1)} collective-permute-done((bf16[280,128]{1,0:T(8,128)(2,1)S(1)}, bf16[280,128]{1,0:T(8,128)(2,1)S(1)}, u32[]{:S(2)}, u32[]{:S(2)}) %collective-permute-start) | collective-permute-done | bytes 71712 | tf_op jit(solution)/shard_map/ppermute | solution.py:389
  26.7 0.0 collective-permute-done.2.refs_1_
  26.7 0.0 collective-permute-done.3.refs_2_
  26.7 1.2 %shard_map.78 = (f32[64,256]{1,0:T(8,128)S(1)}, f32[64,256]{1,0:T(8,128)S(1)}) custom-call(bf16[264,512]{1,0:T(8,128)(2,1)S(1)} %shard_map.73.whole.refs_0_, bf16[264,512]{1,0:T(8,128)(2,1)S(1)} %collective-permute-done.2.refs_1_, bf16[264,512]{1,0:T(8,128)(2,1)S(1)} %collective-permute-done.3.refs_2_, ...), custom_call_target="tpu_custom_call" | custom-call | tf_op jit(solution)/shard_map/pallas_call | solution.py:215
  28.0 0.6 collective-permute-start.4
  28.5 1.2 %collective-permute-start.5 = (f32[64,256]{1,0:T(8,128)S(1)}, f32[64,256]{1,0:T(8,128)S(1)}, u32[]{:S(2)}, u32[]{:S(2)}) collective-permute-start(f32[64,256]{1,0:T(8,128)S(1)} %get-tuple-element.32), channel_id=1, source_target_pairs={{4,8},{12,16},{20,24},{28,0},{8,4},{16,12},{24,20},{0,28},{5,9},{1... | collective-permute-start | bytes 196616 | tf_op jit(solution)/shard_map/ppermute | solution.py:384
  29.7 2.7 %shard_map.76 = (f32[512,256]{1,0:T(8,128)S(1)}, f32[1,512]{1,0:T(1,128)S(1)}) custom-call(bf16[264,512]{1,0:T(8,128)(2,1)S(1)} %shard_map.73.whole.refs_0_, bf16[264,512]{1,0:T(8,128)(2,1)S(1)} %collective-permute-done.2.refs_1_, bf16[264,512]{1,0:T(8,128)(2,1)S(1)} %collective-permute-done.3.refs_2_, ...), custom_call_target="tpu_custom_call" | custom-call | tf_op jit(solution)/shard_map/pallas_call | solution.py:241
  32.4 0.0 collective-permute-done.1.refs_1_
  32.4 1.1 %shard_map.77.main = f32[512,256]{1,0:T(8,128)S(1)} custom-call(bf16[280,128]{1,0:T(8,128)(2,1)S(1)} %collective-permute-done.refs_3_.refs_0_, bf16[256,384]{1,0:T(8,128)(2,1)S(1)} %collective-permute-done.1.refs_1_, bf16[9,256,1024]{2,1,0:T(8,128)(2,1)S(1)} %shard_map.75.refs_4_.refs_2_, ...), custom_call_target="tpu_custom_call", output_to_operand_aliasing={{}: (4, {})} | custom-call | tf_op jit(solution)/shard_map/pallas_call | solution.py:265
  33.6 0.0 collective-permute-done.4.first
  33.6 0.0 collective-permute-done.5.second
  33.6 0.2 shard_map.79
  33.8 2.2 %collective-permute-start.6 = (f32[1,512]{1,0:T(1,128)S(1)}, f32[1,512]{1,0:T(1,128)S(1)}, u32[]{:S(2)}, u32[]{:S(2)}) collective-permute-start(f32[1,512]{1,0:T(1,128)S(1)} %get-tuple-element.34.refs_2_), channel_id=1, source_target_pairs={{0,3},{1,2},{2,1},{3,0},{4,7},{5,6},{6,5},{7,4},{8,11},{9,10},{10,... | collective-permute-start | bytes 6152 | tf_op jit(solution)/shard_map/ppermute | solution.py:389
  36.0 0.0 collective-permute-start.7
  36.1 1.3 %collective-permute-start.8 = (f32[1,512]{1,0:T(1,128)S(1)}, f32[1,512]{1,0:T(1,128)S(1)}, u32[]{:S(2)}, u32[]{:S(2)}) collective-permute-start(f32[1,512]{1,0:T(1,128)S(1)} %get-tuple-element.34.refs_2_), channel_id=1, source_target_pairs={{0,1},{1,0},{2,3},{3,2},{4,5},{5,4},{6,7},{7,6},{8,9},{9,8},{10,11... | collective-permute-start | bytes 6152 | tf_op jit(solution)/shard_map/ppermute | solution.py:389
  37.3 0.0 collective-permute-done.6.refs_3_
  37.3 2.1 %collective-permute-done.7.refs_4_ = f32[1,512]{1,0:T(1,128)S(1)} collective-permute-done((f32[1,512]{1,0:T(1,128)S(1)}, f32[1,512]{1,0:T(1,128)S(1)}, u32[]{:S(2)}, u32[]{:S(2)}) %collective-permute-start.7) | collective-permute-done | bytes 2080 | tf_op jit(solution)/shard_map/ppermute | solution.py:389
  39.4 0.0 collective-permute-done.8.refs_5_
  39.4 0.0 copy-done.2
  39.4 0.3 shard_map.80
  39.7 1.8 %collective-permute-start.12 = (bf16[512,256]{1,0:T(8,128)(2,1)S(1)}, bf16[512,256]{1,0:T(8,128)(2,1)S(1)}, u32[]{:S(2)}, u32[]{:S(2)}) collective-permute-start(bf16[512,256]{1,0:T(8,128)(2,1)S(1)} %get-tuple-element.37.refs_0_), channel_id=1, source_target_pairs={{0,2},{1,3},{2,0},{3,1},{4,6},{5,7},{6,4},{7,5},{8,10},{9,11},{10,... | collective-permute-start | bytes 786440 | tf_op jit(solution)/shard_map/ppermute | solution.py:389
  41.6 0.0 collective-permute-start.11
  41.6 0.9 %collective-permute-start.10 = (bf16[384,256]{1,0:T(8,128)(2,1)S(1)}, bf16[384,256]{1,0:T(8,128)(2,1)S(1)}, u32[]{:S(2)}, u32[]{:S(2)}) collective-permute-start(bf16[384,256]{1,0:T(8,128)(2,1)S(1)} %get-tuple-element.36), channel_id=1, source_target_pairs={{0,3},{1,2},{2,1},{3,0},{4,7},{5,6},{6,5},{7,4},{8,11},{9,10},{10,... | collective-permute-start | bytes 589832 | tf_op jit(solution)/shard_map/ppermute | solution.py:389
  42.4 0.6 collective-permute-start.9
  43.0 2.4 %shard_map.81.refs_1_.refs_2_ = bf16[9,256,1024]{2,1,0:T(8,128)(2,1)S(1)} custom-call(bf16[3,3,3,256,1024]{4,3,2,1,0:T(8,128)(2,1)} %refs_0_.3), custom_call_target="tpu_custom_call" | custom-call | tf_op jit(solution)/shard_map/pallas_call | solution.py:53
  45.4 0.0 copy-start
  45.4 0.0 copy-start.3
  45.4 1.0 %shard_map.82 = (f32[512,256]{1,0:T(8,128)S(1)}, f32[64,256]{1,0:T(8,128)S(1)}, f32[64,256]{1,0:T(8,128)S(1)}) custom-call(bf16[512,256]{1,0:T(8,128)(2,1)S(1)} %get-tuple-element.37.refs_0_, bf16[9,256,1024]{2,1,0:T(8,128)(2,1)S(1)} %shard_map.81.refs_1_.refs_2_), custom_call_target="tpu_custom_call" | custom-call | tf_op jit(solution)/shard_map/pallas_call | solution.py:286
  46.5 7.5 %collective-permute-done.12.refs_0_ = bf16[512,256]{1,0:T(8,128)(2,1)S(1)} collective-permute-done((bf16[512,256]{1,0:T(8,128)(2,1)S(1)}, bf16[512,256]{1,0:T(8,128)(2,1)S(1)}, u32[]{:S(2)}, u32[]{:S(2)}) %collective-permute-start.12) | collective-permute-done | bytes 262176 | tf_op jit(solution)/shard_map/ppermute | solution.py:389
  54.0 1.0 %shard_map.83 = (f32[512,256]{1,0:T(8,128)S(1)}, f32[64,256]{1,0:T(8,128)S(1)}, f32[64,256]{1,0:T(8,128)S(1)}) custom-call(bf16[512,256]{1,0:T(8,128)(2,1)S(1)} %collective-permute-done.12.refs_0_, bf16[9,256,1024]{2,1,0:T(8,128)(2,1)S(1)} %shard_map.81.refs_1_.refs_2_, ...), custom_call_target="tpu_custom_call", output_to_operand_aliasing={{0}: (2, {}), {1}: (3, {}), {2}: (4, {})} | custom-call | tf_op jit(solution)/shard_map/pallas_call | solution.py:286
  55.0 0.0 collective-permute-done.11.refs_0_
  55.0 1.1 %shard_map.84 = (f32[512,256]{1,0:T(8,128)S(1)}, f32[64,256]{1,0:T(8,128)S(1)}, f32[64,256]{1,0:T(8,128)S(1)}) custom-call(bf16[512,256]{1,0:T(8,128)(2,1)S(1)} %collective-permute-done.11.refs_0_, bf16[9,256,1024]{2,1,0:T(8,128)(2,1)S(1)} %shard_map.81.refs_1_.refs_2_, ...), custom_call_target="tpu_custom_call", output_to_operand_aliasing={{0}: (2, {}), {1}: (3, {}), {2}: (4, {})} | custom-call | tf_op jit(solution)/shard_map/pallas_call | solution.py:286
  56.1 8.6 %collective-permute-done.9.refs_0_ = bf16[128,256]{1,0:T(8,128)(2,1)S(1)} collective-permute-done((bf16[128,256]{1,0:T(8,128)(2,1)S(1)}, bf16[128,256]{1,0:T(8,128)(2,1)S(1)}, u32[]{:S(2)}, u32[]{:S(2)}) %collective-permute-start.9) | collective-permute-done | bytes 65568 | tf_op jit(solution)/shard_map/ppermute | solution.py:389
  64.7 0.4 shard_map.86
  65.1 1.1 %collective-permute-start.13 = (f32[64,256]{1,0:T(8,128)S(1)}, f32[64,256]{1,0:T(8,128)S(1)}, u32[]{:S(2)}, u32[]{:S(2)}) collective-permute-start(f32[64,256]{1,0:T(8,128)S(1)} %get-tuple-element.47), channel_id=1, source_target_pairs={{0,4},{8,12},{16,20},{24,28},{4,0},{12,8},{20,16},{28,24},{1,5},{9... | collective-permute-start | bytes 196616 | tf_op jit(solution)/shard_map/ppermute | solution.py:384
  66.2 0.9 %collective-permute-start.14 = (f32[64,256]{1,0:T(8,128)S(1)}, f32[64,256]{1,0:T(8,128)S(1)}, u32[]{:S(2)}, u32[]{:S(2)}) collective-permute-start(f32[64,256]{1,0:T(8,128)S(1)} %get-tuple-element.48), channel_id=1, source_target_pairs={{4,8},{12,16},{20,24},{28,0},{8,4},{16,12},{24,20},{0,28},{5,9},{1... | collective-permute-start | bytes 196616 | tf_op jit(solution)/shard_map/ppermute | solution.py:384
  67.1 0.0 collective-permute-done.10.refs_1_
  67.1 0.8 %shard_map.85.main = f32[512,256]{1,0:T(8,128)S(1)} custom-call(bf16[128,256]{1,0:T(8,128)(2,1)S(1)} %collective-permute-done.9.refs_0_, bf16[384,256]{1,0:T(8,128)(2,1)S(1)} %collective-permute-done.10.refs_1_, bf16[9,256,1024]{2,1,0:T(8,128)(2,1)S(1)} %shard_map.81.refs_1_.refs_2_, ...), custom_call_target="tpu_custom_call", output_to_operand_aliasing={{}: (3, {})} | custom-call | tf_op jit(solution)/shard_map/pallas_call | solution.py:318
  67.9 0.0 collective-permute-done.13.first
  67.9 2.9 %collective-permute-done.14.second = f32[64,256]{1,0:T(8,128)S(1)} collective-permute-done((f32[64,256]{1,0:T(8,128)S(1)}, f32[64,256]{1,0:T(8,128)S(1)}, u32[]{:S(2)}, u32[]{:S(2)}) %collective-permute-start.14) | collective-permute-done | bytes 65568 | tf_op jit(solution)/shard_map/ppermute | solution.py:384
  70.8 0.9 %shard_map.87 = bf16[256,512]{1,0:T(8,128)(2,1)} custom-call(f32[512,256]{1,0:T(8,128)S(1)} %shard_map.85.main, f32[64,256]{1,0:T(8,128)S(1)} %collective-permute-done.13.first, f32[64,256]{1,0:T(8,128)S(1)} %collective-permute-done.14.second, f32[1,256]{1,0:T(1,128)S(1)} %bitcast.10, bf16[256,512]{1,0:T(8,128)(2,1)S(1)} %bitcast.7), custom_call_target="tpu_custom_call" | custom-call | tf_op jit(solution)/shard_map/pallas_call | solution.py:432
  (5 shorter events, 0.0 us)
Async XLA Ops:
  1.0 25.8 %collective-permute-start.2 = (bf16[264,512]{1,0:T(8,128)(2,1)S(1)}, bf16[264,512]{1,0:T(8,128)(2,1)S(1)}, u32[]{:S(2)}, u32[]{:S(2)}) collective-permute-start(bf16[264,512]{1,0:T(8,128)(2,1)S(1)} %shard_map.73.whole.refs_0_), channel_id=1, source_target_pairs={{0,2},{1,3},{2,0},{3,1},{4,6},{5,7},{6,4},{7,5},{8,10},{9,11},{10,... | collective-permute-start | bytes 811016 | tf_op jit(solution)/shard_map/ppermute | solution.py:389
  3.3 23.4 %collective-permute-start.3 = (bf16[264,512]{1,0:T(8,128)(2,1)S(1)}, bf16[264,512]{1,0:T(8,128)(2,1)S(1)}, u32[]{:S(2)}, u32[]{:S(2)}) collective-permute-start(bf16[264,512]{1,0:T(8,128)(2,1)S(1)} %shard_map.73.whole.refs_0_), channel_id=1, source_target_pairs={{0,1},{1,0},{2,3},{3,2},{4,5},{5,4},{6,7},{7,6},{8,9},{9,8},{10,11... | collective-permute-start | bytes 811016 | tf_op jit(solution)/shard_map/ppermute | solution.py:389
  3.7 28.8 %collective-permute-start.1 = (bf16[256,384]{1,0:T(8,128)(2,1)S(1)}, bf16[256,384]{1,0:T(8,128)(2,1)S(1)}, u32[]{:S(2)}, u32[]{:S(2)}) collective-permute-start(bf16[256,384]{1,0:T(8,128)(2,1)S(1)} %get-tuple-element.28), channel_id=1, source_target_pairs={{0,3},{1,2},{2,1},{3,0},{4,7},{5,6},{6,5},{7,4},{8,11},{9,10},{10,... | collective-permute-start | bytes 589832 | tf_op jit(solution)/shard_map/ppermute | solution.py:389
  3.9 29.7 %copy-start.1 = (f32[256]{0:T(256)S(1)}, f32[256]{0:T(256)}, u32[]{:S(2)}) copy-start(f32[256]{0:T(256)} %param.10) | copy-start | bytes 3076
  3.9 35.5 %copy-start.2 = (f32[256]{0:T(256)S(1)}, f32[256]{0:T(256)}, u32[]{:S(2)}) copy-start(f32[256]{0:T(256)} %param.11) | copy-start | bytes 3076
  3.9 22.8 %collective-permute-start = (bf16[280,128]{1,0:T(8,128)(2,1)S(1)}, bf16[280,128]{1,0:T(8,128)(2,1)S(1)}, u32[]{:S(2)}, u32[]{:S(2)}) collective-permute-start(bf16[280,128]{1,0:T(8,128)(2,1)S(1)} %get-tuple-element.27), channel_id=1, source_target_pairs={{0,3},{1,2},{2,1},{3,0},{4,7},{5,6},{6,5},{7,4},{8,11},{9,10},{10,... | collective-permute-start | bytes 215048 | tf_op jit(solution)/shard_map/ppermute | solution.py:389
  28.0 5.6 %collective-permute-start.4 = (f32[64,256]{1,0:T(8,128)S(1)}, f32[64,256]{1,0:T(8,128)S(1)}, u32[]{:S(2)}, u32[]{:S(2)}) collective-permute-start(f32[64,256]{1,0:T(8,128)S(1)} %get-tuple-element.31), channel_id=1, source_target_pairs={{0,4},{8,12},{16,20},{24,28},{4,0},{12,8},{20,16},{28,24},{1,5},{9... | collective-permute-start | bytes 196616 | tf_op jit(solution)/shard_map/ppermute | solution.py:384
  28.5 5.1 %collective-permute-start.5 = (f32[64,256]{1,0:T(8,128)S(1)}, f32[64,256]{1,0:T(8,128)S(1)}, u32[]{:S(2)}, u32[]{:S(2)}) collective-permute-start(f32[64,256]{1,0:T(8,128)S(1)} %get-tuple-element.32), channel_id=1, source_target_pairs={{4,8},{12,16},{20,24},{28,0},{8,4},{16,12},{24,20},{0,28},{5,9},{1... | collective-permute-start | bytes 196616 | tf_op jit(solution)/shard_map/ppermute | solution.py:384
  33.8 3.5 %collective-permute-start.6 = (f32[1,512]{1,0:T(1,128)S(1)}, f32[1,512]{1,0:T(1,128)S(1)}, u32[]{:S(2)}, u32[]{:S(2)}) collective-permute-start(f32[1,512]{1,0:T(1,128)S(1)} %get-tuple-element.34.refs_2_), channel_id=1, source_target_pairs={{0,3},{1,2},{2,1},{3,0},{4,7},{5,6},{6,5},{7,4},{8,11},{9,10},{10,... | collective-permute-start | bytes 6152 | tf_op jit(solution)/shard_map/ppermute | solution.py:389
  36.0 3.3 %collective-permute-start.7 = (f32[1,512]{1,0:T(1,128)S(1)}, f32[1,512]{1,0:T(1,128)S(1)}, u32[]{:S(2)}, u32[]{:S(2)}) collective-permute-start(f32[1,512]{1,0:T(1,128)S(1)} %get-tuple-element.34.refs_2_), channel_id=1, source_target_pairs={{0,2},{1,3},{2,0},{3,1},{4,6},{5,7},{6,4},{7,5},{8,10},{9,11},{10,... | collective-permute-start | bytes 6152 | tf_op jit(solution)/shard_map/ppermute | solution.py:389
  36.1 3.3 %collective-permute-start.8 = (f32[1,512]{1,0:T(1,128)S(1)}, f32[1,512]{1,0:T(1,128)S(1)}, u32[]{:S(2)}, u32[]{:S(2)}) collective-permute-start(f32[1,512]{1,0:T(1,128)S(1)} %get-tuple-element.34.refs_2_), channel_id=1, source_target_pairs={{0,1},{1,0},{2,3},{3,2},{4,5},{5,4},{6,7},{7,6},{8,9},{9,8},{10,11... | collective-permute-start | bytes 6152 | tf_op jit(solution)/shard_map/ppermute | solution.py:389
  39.7 14.2 %collective-permute-start.12 = (bf16[512,256]{1,0:T(8,128)(2,1)S(1)}, bf16[512,256]{1,0:T(8,128)(2,1)S(1)}, u32[]{:S(2)}, u32[]{:S(2)}) collective-permute-start(bf16[512,256]{1,0:T(8,128)(2,1)S(1)} %get-tuple-element.37.refs_0_), channel_id=1, source_target_pairs={{0,2},{1,3},{2,0},{3,1},{4,6},{5,7},{6,4},{7,5},{8,10},{9,11},{10,... | collective-permute-start | bytes 786440 | tf_op jit(solution)/shard_map/ppermute | solution.py:389
  41.6 13.5 %collective-permute-start.11 = (bf16[512,256]{1,0:T(8,128)(2,1)S(1)}, bf16[512,256]{1,0:T(8,128)(2,1)S(1)}, u32[]{:S(2)}, u32[]{:S(2)}) collective-permute-start(bf16[512,256]{1,0:T(8,128)(2,1)S(1)} %get-tuple-element.37.refs_0_), channel_id=1, source_target_pairs={{0,1},{1,0},{2,3},{3,2},{4,5},{5,4},{6,7},{7,6},{8,9},{9,8},{10,11... | collective-permute-start | bytes 786440 | tf_op jit(solution)/shard_map/ppermute | solution.py:389
  41.6 25.5 %collective-permute-start.10 = (bf16[384,256]{1,0:T(8,128)(2,1)S(1)}, bf16[384,256]{1,0:T(8,128)(2,1)S(1)}, u32[]{:S(2)}, u32[]{:S(2)}) collective-permute-start(bf16[384,256]{1,0:T(8,128)(2,1)S(1)} %get-tuple-element.36), channel_id=1, source_target_pairs={{0,3},{1,2},{2,1},{3,0},{4,7},{5,6},{6,5},{7,4},{8,11},{9,10},{10,... | collective-permute-start | bytes 589832 | tf_op jit(solution)/shard_map/ppermute | solution.py:389
  42.4 22.3 %collective-permute-start.9 = (bf16[128,256]{1,0:T(8,128)(2,1)S(1)}, bf16[128,256]{1,0:T(8,128)(2,1)S(1)}, u32[]{:S(2)}, u32[]{:S(2)}) collective-permute-start(bf16[128,256]{1,0:T(8,128)(2,1)S(1)} %get-tuple-element.35), channel_id=1, source_target_pairs={{0,3},{1,2},{2,1},{3,0},{4,7},{5,6},{6,5},{7,4},{8,11},{9,10},{10,... | collective-permute-start | bytes 196616 | tf_op jit(solution)/shard_map/ppermute | solution.py:389
  45.4 25.4 %copy-start = (bf16[256,1,512]{2,0,1:T(8,128)(2,1)S(1)}, bf16[256,1,512]{2,0,1:T(8,128)(2,1)}, u32[]{:S(2)}) copy-start(bf16[256,1,512]{2,0,1:T(8,128)(2,1)} %param.7) | copy-start | bytes 786436
  45.4 25.4 %copy-start.3 = (f32[256]{0:T(256)S(1)}, f32[256]{0:T(256)}, u32[]{:S(2)}) copy-start(f32[256]{0:T(256)} %param.13) | copy-start | bytes 3076
  65.1 2.8 %collective-permute-start.13 = (f32[64,256]{1,0:T(8,128)S(1)}, f32[64,256]{1,0:T(8,128)S(1)}, u32[]{:S(2)}, u32[]{:S(2)}) collective-permute-start(f32[64,256]{1,0:T(8,128)S(1)} %get-tuple-element.47), channel_id=1, source_target_pairs={{0,4},{8,12},{16,20},{24,28},{4,0},{12,8},{20,16},{28,24},{1,5},{9... | collective-permute-start | bytes 196616 | tf_op jit(solution)/shard_map/ppermute | solution.py:384
  66.2 4.6 %collective-permute-start.14 = (f32[64,256]{1,0:T(8,128)S(1)}, f32[64,256]{1,0:T(8,128)S(1)}, u32[]{:S(2)}, u32[]{:S(2)}) collective-permute-start(f32[64,256]{1,0:T(8,128)S(1)} %get-tuple-element.48), channel_id=1, source_target_pairs={{4,8},{12,16},{20,24},{28,0},{8,4},{16,12},{24,20},{0,28},{5,9},{1... | collective-permute-start | bytes 196616 | tf_op jit(solution)/shard_map/ppermute | solution.py:384

commit v3 on v2

--- a/solution.py
+++ b/solution.py
@@ -354,24 +354,35 @@
 
 
 def act_kernel(total, values, gain, *refs):
-    sums, (out, edge, body) = refs[:-3], refs[-3:]
+    sums, out = refs[:-1], refs[-1]
     inverse = column_of(1.0 / jnp.sqrt(sum(ref[...] for ref in sums) / total + 1e-6))
     result = silu(values[...] * gain[...] * inverse).astype(out.dtype)
-    end = result.shape[0] - WIDTH
     out[...] = result
-    edge[:WIDTH], edge[WIDTH:] = result[:WIDTH], result[end:]
-    body[...] = result[WIDTH:end]
+
+
+def cut_kernel(block, edge, body):
+    end = block.shape[0] - WIDTH
+    edge[:WIDTH], edge[WIDTH:] = block[:WIDTH], block[end:]
+    body[...] = block[WIDTH:end]
+
+
+def cut(block):
+    cells, width = block.shape
+    return pl.pallas_call(
+        cut_kernel,
+        out_shape=[jax.ShapeDtypeStruct((n, width), block.dtype) for n in (2 * WIDTH, cells - 2 * WIDTH)],
+        in_specs=[VMEM],
+        out_specs=[VMEM] * 2,
+        compiler_params=PARAMS,
+    )(block)
 
 
 def act(values, gain, sums, total):
     return pl.pallas_call(
         lambda *refs: act_kernel(total, *refs),
-        out_shape=[
-            jax.ShapeDtypeStruct((size, values.shape[1]), jnp.bfloat16)
-            for size in (values.shape[0], 2 * WIDTH, values.shape[0] - 2 * WIDTH)
-        ],
+        out_shape=jax.ShapeDtypeStruct(values.shape, jnp.bfloat16),
         in_specs=[VMEM] * (2 + len(sums)),
-        out_specs=[VMEM] * 3,
+        out_specs=VMEM,
         compiler_params=PARAMS,
     )(values, gain, *sums)
 
@@ -422,7 +433,7 @@
     others = [swap(squares, step) for step in range(count - 1, 0, -1)]
     second = act(middle, gain_second.reshape(1, -1), [squares, *others], total)
     taps = fetch(weight_second)
-    blocks, edge, body = gathered(*second)
+    blocks, edge, body = gathered(second, *cut(second))
     parts = ()
     for k, block in enumerate(blocks):
         parts = second_part(k, block, taps, parts)

time: 71.9 us -> 71.9 us (level)
  no operation moved by 1% of the time
where the time goes in v3:
time: 71.9 us; the launch traced here: 71.7 us
  waiting for transfers between devices  40.1 us (56%)
  Pallas kernels  16.7 us (23%)
  starting transfers between devices  14.6 us (20%)
    ppermute x11, waiting for transfers between devices, swap(): lax.ppermute(value, 'chan', [(i, i ^ step) for i in range(lax.axis_size('...  37.3 us
    ppermute x11, starting transfers between devices, swap(): lax.ppermute(value, 'chan', [(i, i ^ step) for i in range(lax.axis_size('...  10.9 us
    pallas_call x2, Pallas kernels, fetch(): pl.pallas_call(lambda *refs: fetch_kernel(weights.shape[0] - 1, *refs), o...  4.76 us
    ppermute x4, starting transfers between devices, with_row_neighbours(): lax.ppermute(send, 'rows', pairs + [(b, a) for a, b in pairs])  3.7 us
    pallas_call x3, Pallas kernels, second_part(): pl.pallas_call(lambda *refs: part_kernel(k, *refs), out_shape=[jax.ShapeD...  3.13 us
    ppermute x4, waiting for transfers between devices, with_row_neighbours(): lax.ppermute(send, 'rows', pairs + [(b, a) for a, b in pairs])  2.86 us
    pallas_call x1, Pallas kernels, first_upper(): pl.pallas_call(lambda *refs: first_upper_kernel(total, *refs), out_shape=...  2.71 us
  transfers between devices with their start and end apart: 15, of which 5 were waited for; matrix products, arithmetic and copies ran while one was open for 0% of the time, Pallas kernels for 20%

profile of v3, /device:TPU:9, one launch (start us, length us, event | category | flops | bytes accessed | tf_op | source)
XLA Modules:
  0.0 71.7 jit_solution(9386821478830279106)
XLA Ops:
  0.0 1.0 %shard_map.73.whole.refs_0_ = bf16[264,512]{1,0:T(8,128)(2,1)S(1)} custom-call(bf16[256,512]{1,0:T(8,128)(2,1)} %bitcast.6, f32[1,256]{1,0:T(1,128)} %bitcast.11), custom_call_target="tpu_custom_call" | custom-call | tf_op jit(solution)/shard_map/pallas_call | solution.py:170
  1.0 2.4 %collective-permute-start.2 = (bf16[264,512]{1,0:T(8,128)(2,1)S(1)}, bf16[264,512]{1,0:T(8,128)(2,1)S(1)}, u32[]{:S(2)}, u32[]{:S(2)}) collective-permute-start(bf16[264,512]{1,0:T(8,128)(2,1)S(1)} %shard_map.73.whole.refs_0_), channel_id=1, source_target_pairs={{0,2},{1,3},{2,0},{3,1},{4,6},{5,7},{6,4},{7,5},{8,10},{9,11},{10,... | collective-permute-start | bytes 811016 | tf_op jit(solution)/shard_map/ppermute | solution.py:400
  3.3 0.2 collective-permute-start.3
  3.5 0.1 shard_map.74
  3.7 0.3 collective-permute-start.1
  3.9 1.3 %collective-permute-start = (bf16[280,128]{1,0:T(8,128)(2,1)S(1)}, bf16[280,128]{1,0:T(8,128)(2,1)S(1)}, u32[]{:S(2)}, u32[]{:S(2)}) collective-permute-start(bf16[280,128]{1,0:T(8,128)(2,1)S(1)} %get-tuple-element.26), channel_id=1, source_target_pairs={{0,3},{1,2},{2,1},{3,0},{4,7},{5,6},{6,5},{7,4},{8,11},{9,10},{10,... | collective-permute-start | bytes 215048 | tf_op jit(solution)/shard_map/ppermute | solution.py:400
  5.2 2.4 %shard_map.75.refs_4_.refs_2_ = bf16[9,256,1024]{2,1,0:T(8,128)(2,1)S(1)} custom-call(bf16[3,3,3,256,1024]{4,3,2,1,0:T(8,128)(2,1)} %refs_0_.2), custom_call_target="tpu_custom_call" | custom-call | tf_op jit(solution)/shard_map/pallas_call | solution.py:53
  7.6 19.1 %collective-permute-done.refs_3_.refs_0_ = bf16[280,128]{1,0:T(8,128)(2,1)S(1)} collective-permute-done((bf16[280,128]{1,0:T(8,128)(2,1)S(1)}, bf16[280,128]{1,0:T(8,128)(2,1)S(1)}, u32[]{:S(2)}, u32[]{:S(2)}) %collective-permute-start) | collective-permute-done | bytes 71712 | tf_op jit(solution)/shard_map/ppermute | solution.py:400
  26.7 0.0 collective-permute-done.2.refs_1_
  26.7 0.0 collective-permute-done.3.refs_2_
  26.7 1.2 %shard_map.78 = (f32[64,256]{1,0:T(8,128)S(1)}, f32[64,256]{1,0:T(8,128)S(1)}) custom-call(bf16[264,512]{1,0:T(8,128)(2,1)S(1)} %shard_map.73.whole.refs_0_, bf16[264,512]{1,0:T(8,128)(2,1)S(1)} %collective-permute-done.2.refs_1_, bf16[264,512]{1,0:T(8,128)(2,1)S(1)} %collective-permute-done.3.refs_2_, ...), custom_call_target="tpu_custom_call" | custom-call | tf_op jit(solution)/shard_map/pallas_call | solution.py:215
  28.0 0.6 collective-permute-start.4
  28.5 1.2 %collective-permute-start.5 = (f32[64,256]{1,0:T(8,128)S(1)}, f32[64,256]{1,0:T(8,128)S(1)}, u32[]{:S(2)}, u32[]{:S(2)}) collective-permute-start(f32[64,256]{1,0:T(8,128)S(1)} %get-tuple-element.31), channel_id=1, source_target_pairs={{4,8},{12,16},{20,24},{28,0},{8,4},{16,12},{24,20},{0,28},{5,9},{1... | collective-permute-start | bytes 196616 | tf_op jit(solution)/shard_map/ppermute | solution.py:395
  29.7 2.7 %shard_map.76 = (f32[512,256]{1,0:T(8,128)S(1)}, f32[1,512]{1,0:T(1,128)S(1)}) custom-call(bf16[264,512]{1,0:T(8,128)(2,1)S(1)} %shard_map.73.whole.refs_0_, bf16[264,512]{1,0:T(8,128)(2,1)S(1)} %collective-permute-done.2.refs_1_, bf16[264,512]{1,0:T(8,128)(2,1)S(1)} %collective-permute-done.3.refs_2_, ...), custom_call_target="tpu_custom_call" | custom-call | tf_op jit(solution)/shard_map/pallas_call | solution.py:241
  32.4 0.0 collective-permute-done.1.refs_1_
  32.4 1.1 %shard_map.77.main = f32[512,256]{1,0:T(8,128)S(1)} custom-call(bf16[280,128]{1,0:T(8,128)(2,1)S(1)} %collective-permute-done.refs_3_.refs_0_, bf16[256,384]{1,0:T(8,128)(2,1)S(1)} %collective-permute-done.1.refs_1_, bf16[9,256,1024]{2,1,0:T(8,128)(2,1)S(1)} %shard_map.75.refs_4_.refs_2_, ...), custom_call_target="tpu_custom_call", output_to_operand_aliasing={{}: (4, {})} | custom-call | tf_op jit(solution)/shard_map/pallas_call | solution.py:265
  33.6 0.0 collective-permute-done.4.first
  33.6 0.0 collective-permute-done.5.second
  33.6 0.2 shard_map.79
  33.8 2.2 %collective-permute-start.6 = (f32[1,512]{1,0:T(1,128)S(1)}, f32[1,512]{1,0:T(1,128)S(1)}, u32[]{:S(2)}, u32[]{:S(2)}) collective-permute-start(f32[1,512]{1,0:T(1,128)S(1)} %get-tuple-element.33.refs_2_), channel_id=1, source_target_pairs={{0,3},{1,2},{2,1},{3,0},{4,7},{5,6},{6,5},{7,4},{8,11},{9,10},{10,... | collective-permute-start | bytes 6152 | tf_op jit(solution)/shard_map/ppermute | solution.py:400
  36.0 0.0 collective-permute-start.7
  36.1 1.3 %collective-permute-start.8 = (f32[1,512]{1,0:T(1,128)S(1)}, f32[1,512]{1,0:T(1,128)S(1)}, u32[]{:S(2)}, u32[]{:S(2)}) collective-permute-start(f32[1,512]{1,0:T(1,128)S(1)} %get-tuple-element.33.refs_2_), channel_id=1, source_target_pairs={{0,1},{1,0},{2,3},{3,2},{4,5},{5,4},{6,7},{7,6},{8,9},{9,8},{10,11... | collective-permute-start | bytes 6152 | tf_op jit(solution)/shard_map/ppermute | solution.py:400
  37.3 0.0 collective-permute-done.6.refs_3_
  37.3 2.1 %collective-permute-done.7.refs_4_ = f32[1,512]{1,0:T(1,128)S(1)} collective-permute-done((f32[1,512]{1,0:T(1,128)S(1)}, f32[1,512]{1,0:T(1,128)S(1)}, u32[]{:S(2)}, u32[]{:S(2)}) %collective-permute-start.7) | collective-permute-done | bytes 2080 | tf_op jit(solution)/shard_map/ppermute | solution.py:400
  39.4 0.0 collective-permute-done.8.refs_5_
  39.4 0.3 shard_map.80.block.refs_0_
  39.7 1.8 %collective-permute-start.12 = (bf16[512,256]{1,0:T(8,128)(2,1)S(1)}, bf16[512,256]{1,0:T(8,128)(2,1)S(1)}, u32[]{:S(2)}, u32[]{:S(2)}) collective-permute-start(bf16[512,256]{1,0:T(8,128)(2,1)S(1)} %shard_map.80.block.refs_0_), channel_id=1, source_target_pairs={{0,2},{1,3},{2,0},{3,1},{4,6},{5,7},{6,4},{7,5},{8,10},{9,11},{10,... | collective-permute-start | bytes 786440 | tf_op jit(solution)/shard_map/ppermute | solution.py:400
  41.6 0.0 collective-permute-start.11
  41.6 1.0 %collective-permute-start.10 = (bf16[384,256]{1,0:T(8,128)(2,1)S(1)}, bf16[384,256]{1,0:T(8,128)(2,1)S(1)}, u32[]{:S(2)}, u32[]{:S(2)}) collective-permute-start(bf16[384,256]{1,0:T(8,128)(2,1)S(1)} %get-tuple-element.35), channel_id=1, source_target_pairs={{0,3},{1,2},{2,1},{3,0},{4,7},{5,6},{6,5},{7,4},{8,11},{9,10},{10,... | collective-permute-start | bytes 589832 | tf_op jit(solution)/shard_map/ppermute | solution.py:400
  42.5 0.6 collective-permute-start.9
  43.1 2.4 %shard_map.82.refs_1_.refs_2_ = bf16[9,256,1024]{2,1,0:T(8,128)(2,1)S(1)} custom-call(bf16[3,3,3,256,1024]{4,3,2,1,0:T(8,128)(2,1)} %refs_0_.3), custom_call_target="tpu_custom_call" | custom-call | tf_op jit(solution)/shard_map/pallas_call | solution.py:53
  45.5 0.0 copy-start
  45.5 0.0 copy-start.3
  45.5 1.0 %shard_map.83 = (f32[512,256]{1,0:T(8,128)S(1)}, f32[64,256]{1,0:T(8,128)S(1)}, f32[64,256]{1,0:T(8,128)S(1)}) custom-call(bf16[512,256]{1,0:T(8,128)(2,1)S(1)} %shard_map.80.block.refs_0_, bf16[9,256,1024]{2,1,0:T(8,128)(2,1)S(1)} %shard_map.82.refs_1_.refs_2_), custom_call_target="tpu_custom_call" | custom-call | tf_op jit(solution)/shard_map/pallas_call | solution.py:286
  46.6 7.4 %collective-permute-done.12.refs_0_ = bf16[512,256]{1,0:T(8,128)(2,1)S(1)} collective-permute-done((bf16[512,256]{1,0:T(8,128)(2,1)S(1)}, bf16[512,256]{1,0:T(8,128)(2,1)S(1)}, u32[]{:S(2)}, u32[]{:S(2)}) %collective-permute-start.12) | collective-permute-done | bytes 262176 | tf_op jit(solution)/shard_map/ppermute | solution.py:400
  54.0 1.0 %shard_map.84 = (f32[512,256]{1,0:T(8,128)S(1)}, f32[64,256]{1,0:T(8,128)S(1)}, f32[64,256]{1,0:T(8,128)S(1)}) custom-call(bf16[512,256]{1,0:T(8,128)(2,1)S(1)} %collective-permute-done.12.refs_0_, bf16[9,256,1024]{2,1,0:T(8,128)(2,1)S(1)} %shard_map.82.refs_1_.refs_2_, ...), custom_call_target="tpu_custom_call", output_to_operand_aliasing={{0}: (2, {}), {1}: (3, {}), {2}: (4, {})} | custom-call | tf_op jit(solution)/shard_map/pallas_call | solution.py:286
  55.0 0.0 collective-permute-done.11.refs_0_
  55.0 1.1 %shard_map.85 = (f32[512,256]{1,0:T(8,128)S(1)}, f32[64,256]{1,0:T(8,128)S(1)}, f32[64,256]{1,0:T(8,128)S(1)}) custom-call(bf16[512,256]{1,0:T(8,128)(2,1)S(1)} %collective-permute-done.11.refs_0_, bf16[9,256,1024]{2,1,0:T(8,128)(2,1)S(1)} %shard_map.82.refs_1_.refs_2_, ...), custom_call_target="tpu_custom_call", output_to_operand_aliasing={{0}: (2, {}), {1}: (3, {}), {2}: (4, {})} | custom-call | tf_op jit(solution)/shard_map/pallas_call | solution.py:286
  56.1 8.6 %collective-permute-done.9.refs_0_ = bf16[128,256]{1,0:T(8,128)(2,1)S(1)} collective-permute-done((bf16[128,256]{1,0:T(8,128)(2,1)S(1)}, bf16[128,256]{1,0:T(8,128)(2,1)S(1)}, u32[]{:S(2)}, u32[]{:S(2)}) %collective-permute-start.9) | collective-permute-done | bytes 65568 | tf_op jit(solution)/shard_map/ppermute | solution.py:400
  64.7 0.4 shard_map.87
  65.1 1.1 %collective-permute-start.13 = (f32[64,256]{1,0:T(8,128)S(1)}, f32[64,256]{1,0:T(8,128)S(1)}, u32[]{:S(2)}, u32[]{:S(2)}) collective-permute-start(f32[64,256]{1,0:T(8,128)S(1)} %get-tuple-element.45), channel_id=1, source_target_pairs={{0,4},{8,12},{16,20},{24,28},{4,0},{12,8},{20,16},{28,24},{1,5},{9... | collective-permute-start | bytes 196616 | tf_op jit(solution)/shard_map/ppermute | solution.py:395
  66.2 0.9 %collective-permute-start.14 = (f32[64,256]{1,0:T(8,128)S(1)}, f32[64,256]{1,0:T(8,128)S(1)}, u32[]{:S(2)}, u32[]{:S(2)}) collective-permute-start(f32[64,256]{1,0:T(8,128)S(1)} %get-tuple-element.46), channel_id=1, source_target_pairs={{4,8},{12,16},{20,24},{28,0},{8,4},{16,12},{24,20},{0,28},{5,9},{1... | collective-permute-start | bytes 196616 | tf_op jit(solution)/shard_map/ppermute | solution.py:395
  67.1 0.0 collective-permute-done.10.refs_1_
  67.1 0.8 %shard_map.86.main = f32[512,256]{1,0:T(8,128)S(1)} custom-call(bf16[128,256]{1,0:T(8,128)(2,1)S(1)} %collective-permute-done.9.refs_0_, bf16[384,256]{1,0:T(8,128)(2,1)S(1)} %collective-permute-done.10.refs_1_, bf16[9,256,1024]{2,1,0:T(8,128)(2,1)S(1)} %shard_map.82.refs_1_.refs_2_, ...), custom_call_target="tpu_custom_call", output_to_operand_aliasing={{}: (3, {})} | custom-call | tf_op jit(solution)/shard_map/pallas_call | solution.py:318
  67.9 0.0 collective-permute-done.13.first
  67.9 2.9 %collective-permute-done.14.second = f32[64,256]{1,0:T(8,128)S(1)} collective-permute-done((f32[64,256]{1,0:T(8,128)S(1)}, f32[64,256]{1,0:T(8,128)S(1)}, u32[]{:S(2)}, u32[]{:S(2)}) %collective-permute-start.14) | collective-permute-done | bytes 65568 | tf_op jit(solution)/shard_map/ppermute | solution.py:395
  70.8 0.0 copy-done.3
  70.8 0.9 %shard_map.88 = bf16[256,512]{1,0:T(8,128)(2,1)} custom-call(f32[512,256]{1,0:T(8,128)S(1)} %shard_map.86.main, f32[64,256]{1,0:T(8,128)S(1)} %collective-permute-done.13.first, f32[64,256]{1,0:T(8,128)S(1)} %collective-permute-done.14.second, f32[1,256]{1,0:T(1,128)S(1)} %bitcast.10, bf16[256,512]{1,0:T(8,128)(2,1)S(1)} %bitcast.7), custom_call_target="tpu_custom_call" | custom-call | tf_op jit(solution)/shard_map/pallas_call | solution.py:443
  (6 shorter events, 0.0 us)
Async XLA Ops:
  1.0 25.8 %collective-permute-start.2 = (bf16[264,512]{1,0:T(8,128)(2,1)S(1)}, bf16[264,512]{1,0:T(8,128)(2,1)S(1)}, u32[]{:S(2)}, u32[]{:S(2)}) collective-permute-start(bf16[264,512]{1,0:T(8,128)(2,1)S(1)} %shard_map.73.whole.refs_0_), channel_id=1, source_target_pairs={{0,2},{1,3},{2,0},{3,1},{4,6},{5,7},{6,4},{7,5},{8,10},{9,11},{10,... | collective-permute-start | bytes 811016 | tf_op jit(solution)/shard_map/ppermute | solution.py:400
  3.3 23.4 %collective-permute-start.3 = (bf16[264,512]{1,0:T(8,128)(2,1)S(1)}, bf16[264,512]{1,0:T(8,128)(2,1)S(1)}, u32[]{:S(2)}, u32[]{:S(2)}) collective-permute-start(bf16[264,512]{1,0:T(8,128)(2,1)S(1)} %shard_map.73.whole.refs_0_), channel_id=1, source_target_pairs={{0,1},{1,0},{2,3},{3,2},{4,5},{5,4},{6,7},{7,6},{8,9},{9,8},{10,11... | collective-permute-start | bytes 811016 | tf_op jit(solution)/shard_map/ppermute | solution.py:400
  3.7 28.8 %collective-permute-start.1 = (bf16[256,384]{1,0:T(8,128)(2,1)S(1)}, bf16[256,384]{1,0:T(8,128)(2,1)S(1)}, u32[]{:S(2)}, u32[]{:S(2)}) collective-permute-start(bf16[256,384]{1,0:T(8,128)(2,1)S(1)} %get-tuple-element.27), channel_id=1, source_target_pairs={{0,3},{1,2},{2,1},{3,0},{4,7},{5,6},{6,5},{7,4},{8,11},{9,10},{10,... | collective-permute-start | bytes 589832 | tf_op jit(solution)/shard_map/ppermute | solution.py:400
  3.9 29.7 %copy-start.1 = (f32[256]{0:T(256)S(1)}, f32[256]{0:T(256)}, u32[]{:S(2)}) copy-start(f32[256]{0:T(256)} %param.10) | copy-start | bytes 3076
  3.9 35.5 %copy-start.2 = (f32[256]{0:T(256)S(1)}, f32[256]{0:T(256)}, u32[]{:S(2)}) copy-start(f32[256]{0:T(256)} %param.11) | copy-start | bytes 3076
  3.9 22.8 %collective-permute-start = (bf16[280,128]{1,0:T(8,128)(2,1)S(1)}, bf16[280,128]{1,0:T(8,128)(2,1)S(1)}, u32[]{:S(2)}, u32[]{:S(2)}) collective-permute-start(bf16[280,128]{1,0:T(8,128)(2,1)S(1)} %get-tuple-element.26), channel_id=1, source_target_pairs={{0,3},{1,2},{2,1},{3,0},{4,7},{5,6},{6,5},{7,4},{8,11},{9,10},{10,... | collective-permute-start | bytes 215048 | tf_op jit(solution)/shard_map/ppermute | solution.py:400
  28.0 5.6 %collective-permute-start.4 = (f32[64,256]{1,0:T(8,128)S(1)}, f32[64,256]{1,0:T(8,128)S(1)}, u32[]{:S(2)}, u32[]{:S(2)}) collective-permute-start(f32[64,256]{1,0:T(8,128)S(1)} %get-tuple-element.30), channel_id=1, source_target_pairs={{0,4},{8,12},{16,20},{24,28},{4,0},{12,8},{20,16},{28,24},{1,5},{9... | collective-permute-start | bytes 196616 | tf_op jit(solution)/shard_map/ppermute | solution.py:395
  28.5 5.1 %collective-permute-start.5 = (f32[64,256]{1,0:T(8,128)S(1)}, f32[64,256]{1,0:T(8,128)S(1)}, u32[]{:S(2)}, u32[]{:S(2)}) collective-permute-start(f32[64,256]{1,0:T(8,128)S(1)} %get-tuple-element.31), channel_id=1, source_target_pairs={{4,8},{12,16},{20,24},{28,0},{8,4},{16,12},{24,20},{0,28},{5,9},{1... | collective-permute-start | bytes 196616 | tf_op jit(solution)/shard_map/ppermute | solution.py:395
  33.8 3.5 %collective-permute-start.6 = (f32[1,512]{1,0:T(1,128)S(1)}, f32[1,512]{1,0:T(1,128)S(1)}, u32[]{:S(2)}, u32[]{:S(2)}) collective-permute-start(f32[1,512]{1,0:T(1,128)S(1)} %get-tuple-element.33.refs_2_), channel_id=1, source_target_pairs={{0,3},{1,2},{2,1},{3,0},{4,7},{5,6},{6,5},{7,4},{8,11},{9,10},{10,... | collective-permute-start | bytes 6152 | tf_op jit(solution)/shard_map/ppermute | solution.py:400
  36.0 3.3 %collective-permute-start.7 = (f32[1,512]{1,0:T(1,128)S(1)}, f32[1,512]{1,0:T(1,128)S(1)}, u32[]{:S(2)}, u32[]{:S(2)}) collective-permute-start(f32[1,512]{1,0:T(1,128)S(1)} %get-tuple-element.33.refs_2_), channel_id=1, source_target_pairs={{0,2},{1,3},{2,0},{3,1},{4,6},{5,7},{6,4},{7,5},{8,10},{9,11},{10,... | collective-permute-start | bytes 6152 | tf_op jit(solution)/shard_map/ppermute | solution.py:400
  36.1 3.3 %collective-permute-start.8 = (f32[1,512]{1,0:T(1,128)S(1)}, f32[1,512]{1,0:T(1,128)S(1)}, u32[]{:S(2)}, u32[]{:S(2)}) collective-permute-start(f32[1,512]{1,0:T(1,128)S(1)} %get-tuple-element.33.refs_2_), channel_id=1, source_target_pairs={{0,1},{1,0},{2,3},{3,2},{4,5},{5,4},{6,7},{7,6},{8,9},{9,8},{10,11... | collective-permute-start | bytes 6152 | tf_op jit(solution)/shard_map/ppermute | solution.py:400
  39.7 14.2 %collective-permute-start.12 = (bf16[512,256]{1,0:T(8,128)(2,1)S(1)}, bf16[512,256]{1,0:T(8,128)(2,1)S(1)}, u32[]{:S(2)}, u32[]{:S(2)}) collective-permute-start(bf16[512,256]{1,0:T(8,128)(2,1)S(1)} %shard_map.80.block.refs_0_), channel_id=1, source_target_pairs={{0,2},{1,3},{2,0},{3,1},{4,6},{5,7},{6,4},{7,5},{8,10},{9,11},{10,... | collective-permute-start | bytes 786440 | tf_op jit(solution)/shard_map/ppermute | solution.py:400
  41.6 13.4 %collective-permute-start.11 = (bf16[512,256]{1,0:T(8,128)(2,1)S(1)}, bf16[512,256]{1,0:T(8,128)(2,1)S(1)}, u32[]{:S(2)}, u32[]{:S(2)}) collective-permute-start(bf16[512,256]{1,0:T(8,128)(2,1)S(1)} %shard_map.80.block.refs_0_), channel_id=1, source_target_pairs={{0,1},{1,0},{2,3},{3,2},{4,5},{5,4},{6,7},{7,6},{8,9},{9,8},{10,11... | collective-permute-start | bytes 786440 | tf_op jit(solution)/shard_map/ppermute | solution.py:400
  41.6 25.5 %collective-permute-start.10 = (bf16[384,256]{1,0:T(8,128)(2,1)S(1)}, bf16[384,256]{1,0:T(8,128)(2,1)S(1)}, u32[]{:S(2)}, u32[]{:S(2)}) collective-permute-start(bf16[384,256]{1,0:T(8,128)(2,1)S(1)} %get-tuple-element.35), channel_id=1, source_target_pairs={{0,3},{1,2},{2,1},{3,0},{4,7},{5,6},{6,5},{7,4},{8,11},{9,10},{10,... | collective-permute-start | bytes 589832 | tf_op jit(solution)/shard_map/ppermute | solution.py:400
  42.5 22.2 %collective-permute-start.9 = (bf16[128,256]{1,0:T(8,128)(2,1)S(1)}, bf16[128,256]{1,0:T(8,128)(2,1)S(1)}, u32[]{:S(2)}, u32[]{:S(2)}) collective-permute-start(bf16[128,256]{1,0:T(8,128)(2,1)S(1)} %get-tuple-element.34), channel_id=1, source_target_pairs={{0,3},{1,2},{2,1},{3,0},{4,7},{5,6},{6,5},{7,4},{8,11},{9,10},{10,... | collective-permute-start | bytes 196616 | tf_op jit(solution)/shard_map/ppermute | solution.py:400
  45.5 25.3 %copy-start = (bf16[256,1,512]{2,0,1:T(8,128)(2,1)S(1)}, bf16[256,1,512]{2,0,1:T(8,128)(2,1)}, u32[]{:S(2)}) copy-start(bf16[256,1,512]{2,0,1:T(8,128)(2,1)} %param.7) | copy-start | bytes 786436
  45.5 25.3 %copy-start.3 = (f32[256]{0:T(256)S(1)}, f32[256]{0:T(256)}, u32[]{:S(2)}) copy-start(f32[256]{0:T(256)} %param.13) | copy-start | bytes 3076
  65.1 2.8 %collective-permute-start.13 = (f32[64,256]{1,0:T(8,128)S(1)}, f32[64,256]{1,0:T(8,128)S(1)}, u32[]{:S(2)}, u32[]{:S(2)}) collective-permute-start(f32[64,256]{1,0:T(8,128)S(1)} %get-tuple-element.45), channel_id=1, source_target_pairs={{0,4},{8,12},{16,20},{24,28},{4,0},{12,8},{20,16},{28,24},{1,5},{9... | collective-permute-start | bytes 196616 | tf_op jit(solution)/shard_map/ppermute | solution.py:395
  66.2 4.6 %collective-permute-start.14 = (f32[64,256]{1,0:T(8,128)S(1)}, f32[64,256]{1,0:T(8,128)S(1)}, u32[]{:S(2)}, u32[]{:S(2)}) collective-permute-start(f32[64,256]{1,0:T(8,128)S(1)} %get-tuple-element.46), channel_id=1, source_target_pairs={{4,8},{12,16},{20,24},{28,0},{8,4},{16,12},{24,20},{0,28},{5,9},{1... | collective-permute-start | bytes 196616 | tf_op jit(solution)/shard_map/ppermute | solution.py:395
